TPU v7x, 512 devices: a whole 4x8x8 slice. The times are simulated.
512 devices in a mesh: seq: 64 (over z, y_hi, core), head: 8 (over x, y_lo).
Axes of the slice: x: 4, y: 8 (y_hi: 4, y_lo: 2; y = y_hi * 2 + y_lo), z: 8, core: 2. Of those that a mesh axis runs over, the one named last changes fastest.
Arguments:
- block_query_rows: bfloat16 [8192, 5120], P('seq', 'head'), may hold values from -180 to 180
- block_key_rows: bfloat16 [8192, 1024], P('seq', 'head'), may hold values from -6 to 6
- block_value_rows: bfloat16 [8192, 1024], P('seq', 'head'), may hold values from -6 to 6
- stretch_segments: int32 [8192], P('seq'), may hold values from 0 to 15, never falling along the last dimension, each value on 1 to 6144 neighbouring positions
- residual: bfloat16 [8192, 5120], P('seq', 'head'), may hold values from -6 to 6
- out_weight: bfloat16 [5120, 5120], P('head', 'seq'), may hold values from -0.25 to 0.25
- cache_by_prefill: bfloat16 [2, 2, 2048, 16, 1024], P(None, None, 'seq', None, 'head'), may hold values from -6 to 6
- request_pages: int32 [128], replicated, may hold values from 1 to 64, as said below
- request_owner: int32 [128], replicated, may hold values from 0 to 63, as said below
Outputs:
- layer_out: bfloat16 [8192, 5120], P('seq', 'head')
- cache_decode: bfloat16 [2, 2, 4096, 16, 1024], P(None, None, 'seq', None, 'head')
Inputs may be any that keep to these rules, and one draw needn't show every extreme that they name: `stretch_segments`: each request of the block holds at most 6144 tokens, and some request exactly that many. `request_pages`: the requests of one decode device hold at most 64 pages together, and those of some device exactly 64. `request_owner`: never falls along the requests; every device owns at least one request.
All inputs are finite; a program needn't handle non-finite values.
Results may differ from a plain program's by a relative error of at most 0.0065.
Values may be sent and summed in bfloat16 or wider, within the bound.
A program may use at most 128 MiB of HBM per device.

v0:
```python
import jax
import jax.numpy as jnp
from jax import lax
from jax.sharding import PartitionSpec as P

HEAD_SIZE = 128


def on_device(
    block_query_rows,
    block_key_rows,
    block_value_rows,
    stretch_segments,
    residual,
    out_weight,
    cache_by_prefill,
    request_pages,
    request_owner,
):
    seq_count = lax.axis_size("seq")
    seq_place = lax.axis_index("seq")
    rows = block_query_rows.shape[0]
    kv_local = block_key_rows.shape[1] // HEAD_SIZE
    query_groups = block_query_rows.shape[1] // block_key_rows.shape[1]
    query_four = block_query_rows.reshape(rows, kv_local, query_groups, HEAD_SIZE)
    query_place = seq_place * rows + jnp.arange(rows, dtype=jnp.int32)
    scale = HEAD_SIZE ** (-0.5)
    key_part = lax.all_gather(block_key_rows, "seq", axis=0, tiled=True)
    value_part = lax.all_gather(block_value_rows, "seq", axis=0, tiled=True)
    segment_part = lax.all_gather(stretch_segments, "seq", axis=0, tiled=True)
    count = key_part.shape[0]
    key_place = jnp.arange(count, dtype=jnp.int32)
    allowed = (
        (stretch_segments[:, None] == segment_part[None, :])
        & (query_place[:, None] >= key_place[None, :])
        & (key_place[None, :] >= 0)
    )
    running_max = jnp.full((kv_local, query_groups, rows), -1e30, jnp.float32)
    key_three = key_part.reshape(count, kv_local, HEAD_SIZE)
    value_three = value_part.reshape(count, kv_local, HEAD_SIZE)
    scores = (
        jnp.einsum("tkgd,pkd->kgtp", query_four, key_three, preferred_element_type=jnp.float32)
        * scale
    )
    masked = jnp.where(allowed, scores, -1e30)
    new_max = jnp.maximum(running_max, jnp.max(masked, axis=-1))
    weights = jnp.where(allowed, jnp.exp(masked - new_max[..., None]), 0.0)
    new_sum = jnp.sum(weights, axis=-1)
    contribution = jnp.einsum(
        "kgtp,pkd->kgtd",
        weights.astype(jnp.bfloat16),
        value_three,
        preferred_element_type=jnp.float32,
    )
    attention = (
        jnp.transpose(contribution / new_sum[..., None], (2, 0, 1, 3))
        .reshape(rows, -1)
        .astype(jnp.bfloat16)
    )
    partial_value = jnp.dot(
        attention,
        lax.all_gather(out_weight, "seq", axis=1, tiled=True),
        preferred_element_type=jnp.float32,
    )
    feature_width = partial_value.shape[1] // lax.axis_size("head")
    total = lax.psum(partial_value.astype(jnp.bfloat16), "head").astype(jnp.float32)
    mine = lax.dynamic_slice_in_dim(total, lax.axis_index("head") * feature_width, feature_width, 1)
    layer_out = (residual.astype(jnp.float32) + mine).astype(jnp.bfloat16)
    local_pages = cache_by_prefill.shape[2]
    capacity = 2 * local_pages
    per_pair = capacity // seq_count
    owners = jnp.arange(seq_count, dtype=jnp.int32)
    run_pages = jnp.sum(
        jnp.where(request_owner[None, :] == owners[:, None], request_pages[None, :], 0), axis=1
    )
    run_start = jnp.sum(
        jnp.where(request_owner[None, :] < owners[:, None], request_pages[None, :], 0), axis=1
    )
    pair_slots = jnp.arange(per_pair, dtype=jnp.int32)
    offset = (seq_place - run_start) % seq_count
    slot_index = pair_slots[None, :] * seq_count + offset[:, None]
    sending = slot_index < run_pages[:, None]
    local_index = pair_slots[None, :] + ((run_start + offset - seq_place) // seq_count)[:, None]
    local_index = jnp.where(sending, local_index, 0).reshape(-1)
    picked = jnp.take(cache_by_prefill, local_index, axis=2)
    outgoing = jnp.where(
        sending.reshape(-1)[None, None, :, None, None], picked, jnp.zeros_like(picked)
    )
    incoming = lax.all_to_all(outgoing, "seq", split_axis=2, concat_axis=2, tiled=True)
    layers, pair_kv, _, page_len, width = incoming.shape
    arranged = jnp.swapaxes(
        incoming.reshape(layers, pair_kv, seq_count, per_pair, page_len, width), 2, 3
    )
    my_start = run_start[seq_place]
    my_pages = run_pages[seq_place]
    rotated = jnp.roll(arranged, -my_start, axis=3).reshape(
        layers, pair_kv, capacity, page_len, width
    )
    keep = jnp.arange(capacity, dtype=jnp.int32) < my_pages
    cache_decode = jnp.where(keep[None, None, :, None, None], rotated, jnp.zeros_like(rotated))
    return (layer_out, cache_decode)


def solution(mesh):
    return jax.shard_map(
        on_device,
        mesh=mesh,
        in_specs=(
            P("seq", "head"),
            P("seq", "head"),
            P("seq", "head"),
            P("seq"),
            P("seq", "head"),
            P("head", "seq"),
            P(None, None, "seq", None, "head"),
            P(),
            P(),
        ),
        out_specs=(P("seq", "head"), P(None, None, "seq", None, "head")),
        check_vma=False,
    )
```

profile of v0, /device:TPU:6, one launch (start us, length us, event | category | flops | bytes accessed | tf_op | source)
XLA Modules:
  0.0 389.7 jit_solution(16656007094815539979)
XLA Ops:
  7.2 0.7 all-gather.5.cloned.1.call-update
  8.0 1.5 copy.27
  9.5 0.7 all-gather.9.cloned.1.call-update
  10.2 0.8 select_reduce_fusion.1
  11.0 0.8 gather_fusion
  11.9 1.2 select_bitcast_fusion
  13.1 16.6 %all-to-all-start = ((bf16[2,2,64,16,128]{4,3,1,0,2:T(8,128)(2,1)}), bf16[2,2,64,16,128]{4,3,1,0,2:T(8,128)(2,1)S(1)}, u32[]{:S(2)}, u32[]{:S(2)}) async-start(bf16[2,2,64,16,128]{4,3,1,0,2:T(8,128)(2,1)} %select_bitcast_fusion), calls=%async_computation | async-start | bytes 2097152 | tf_op jit(solution)/shard_map/all_to_all | solution.py:89
  29.7 0.0 all-reduce.2.cloned.1.call-start
  29.7 1.1 copy.25
  30.8 99.6 %all-gather = s32[64,1,128]{2,1,0:T(1,128)S(1)} all-gather(s32[1,1,128]{2,1,0:T(1,128)} %bitcast.79), channel_id=1, replica_groups=mesh['seq'=64,'head'=8] {'seq'}, dimensions={0}, use_global_device_ids=true | all-gather | bytes 33280 | tf_op jit(solution)/shard_map/all_gather | solution.py:30
  130.4 4.4 %fusion.7 = pred[128,8192]{0,1:T(8,128)(4,1)S(1)} fusion(s32[128]{0:T(128)S(1)} %iota_add_fusion, s32[128]{0:T(128)} %param.12, s32[8192]{0:T(1024)S(1)} %bitcast.78), kind=kLoop, calls=%fused_computation.11 | loop fusion | flops 3145728 | bytes 1082368 | tf_op jit(solution)/shard_map/and | solution.py:34
  134.8 4.7 %fusion = (f32[5,128]{1,0:T(8,128)S(1)}, f32[8192,128,5]{1,0,2:T(8,128)S(1)}) fusion(pred[128,8192]{0,1:T(8,128)(4,1)S(1)} %fusion.7, bf16[128,5,128]{0,2,1:T(8,128)(2,1)S(1)} %bitcast.76, bf16[8192,128]{1,0:T(8,128)(2,1)} %all-gather.5.cloned.1.call-done), kind=kOutput, calls=%fused_computation.3 | convolution fusion | flops 1357905280 | bytes 24283648 | tf_op jit(solution)/shard_map/tkgd,pkd->kgtp/dot_general | solution.py:42
  139.6 6.9 %copy-done.1 = f32[8192,128,5]{1,0,2:T(8,128)} copy-done((f32[8192,128,5]{1,0,2:T(8,128)}, f32[8192,128,5]{1,0,2:T(8,128)S(1)}, u32[]{:S(2)}) %copy-start.1) | copy-done | bytes 20971544
  146.5 5.2 %fusion.1 = f32[5,128]{1,0:T(8,128)S(1)} fusion(f32[8192,128,5]{1,0,2:T(8,128)S(1)} %get-tuple-element.7, f32[5,128]{1,0:T(8,128)S(1)} %broadcast_maximum_fusion, pred[128,8192]{0,1:T(8,128)(4,1)S(1)} %fusion.7), kind=kLoop, calls=%fused_computation.4 | loop fusion | flops 26213760 | bytes 22025216 | tf_op jit(solution)/shard_map/reduce_sum | solution.py:48
  151.7 39.6 %all-gather.7.cloned.1.call-done = bf16[8192,128]{0,1:T(8,128)(2,1)} async-done(((bf16[128,128]{0,1:T(8,128)(2,1)}), bf16[8192,128]{0,1:T(8,128)(2,1)}) %all-gather.7.cloned.1.call-update) | async-done | bytes 2097168 | tf_op jit(solution)/shard_map/all_gather | solution.py:29
  191.3 12.9 %fusion.16 = bf16[5,128,128]{1,2,0:T(8,128)(2,1)S(1)} fusion(f32[8192,128,5]{1,0,2:T(8,128)} %copy-done.1, f32[5,128]{1,0:T(8,128)S(1)} %broadcast_maximum_fusion, pred[128,8192]{0,1:T(8,128)(4,1)S(1)} %fusion.7, bf16[8192,128]{0,1:T(8,128)(2,1)} %all-gather.7.cloned.1.call-done, f32[5,128]{1,0:T(8,128)S(1)} %fusion.1), kind=kOutput, calls=%fused_computation.18 | convolution fusion | flops 1368555520 | bytes 24286208 | tf_op jit(solution)/shard_map/kgtp,pkd->kgtd/dot_general | solution.py:49
  204.2 83.6 %all-gather.9.cloned.1.call-done = bf16[640,5120]{0,1:T(8,128)(2,1)} async-done(((bf16[640,80]{0,1:T(8,128)(2,1)}), bf16[640,5120]{0,1:T(8,128)(2,1)}) %all-gather.9.cloned.1.call-update) | async-done | bytes 6553616 | tf_op jit(solution)/shard_map/all_gather | solution.py:62
  287.8 6.2 %convolution_convert_fusion = bf16[128,5120]{1,0:T(8,128)(2,1)} fusion(bf16[128,640]{0,1:T(8,128)(2,1)S(1)} %bitcast.77, bf16[640,5120]{0,1:T(8,128)(2,1)} %all-gather.9.cloned.1.call-done), kind=kOutput, calls=%fused_computation.9 | convolution fusion | flops 839516160 | bytes 8028160 | tf_op jit(solution)/shard_map/dot_general | solution.py:60
  294.0 0.6 dynamic_slice.14
  294.6 0.6 dynamic_slice.15
  296.5 0.7 iota_compare_fusion.3
  297.2 1.5 bitcast_select_fusion.1
  298.7 82.9 %all-reduce.2.cloned.1.call-done = bf16[128,5120]{1,0:T(8,128)(2,1)} async-done(((bf16[128,5120]{1,0:T(8,128)(2,1)}), bf16[128,5120]{1,0:T(8,128)(2,1)}) %all-reduce.2.cloned.1.call-update) | async-done | bytes 1310736 | tf_op jit(solution)/shard_map/psum | solution.py:66
  381.6 1.6 add_convert_fusion
  (17 shorter events, 0.3 us)
Async XLA Ops:
  7.2 3.9 copy-start
  7.2 127.6 %all-gather.5.cloned.1.call-start = ((), (), s32[]{:S(2)}) async-start(), calls=%async_computation.1 | async-start | bytes 2129920 | tf_op jit(solution)/shard_map/all_gather | solution.py:28
  7.9 183.4 %all-gather.7.cloned.1.call-start = ((), (), s32[]{:S(2)}) async-start(), calls=%async_computation.2 | async-start | bytes 2129920 | tf_op jit(solution)/shard_map/all_gather | solution.py:29
  9.5 278.3 %all-gather.9.cloned.1.call-start = ((), (), s32[]{:S(2)}) async-start(), calls=%async_computation.3 | async-start | bytes 6656000 | tf_op jit(solution)/shard_map/all_gather | solution.py:62
  13.1 284.1 %all-to-all-start = ((bf16[2,2,64,16,128]{4,3,1,0,2:T(8,128)(2,1)}), bf16[2,2,64,16,128]{4,3,1,0,2:T(8,128)(2,1)S(1)}, u32[]{:S(2)}, u32[]{:S(2)}) async-start(bf16[2,2,64,16,128]{4,3,1,0,2:T(8,128)(2,1)} %select_bitcast_fusion), calls=%async_computation | async-start | bytes 2097152 | tf_op jit(solution)/shard_map/all_to_all | solution.py:89
  29.7 351.9 %all-reduce.2.cloned.1.call-start = ((), (), s32[]{:S(2)}) async-start(), calls=%async_computation.4 | async-start | bytes 2621440 | tf_op jit(solution)/shard_map/psum | solution.py:66
  139.6 7.0 %copy-start.1 = (f32[8192,128,5]{1,0,2:T(8,128)}, f32[8192,128,5]{1,0,2:T(8,128)S(1)}, u32[]{:S(2)}) copy-start(f32[8192,128,5]{1,0,2:T(8,128)S(1)} %get-tuple-element.7) | copy-start | bytes 62914564
  204.2 177.3 %copy-start.2 = (bf16[128,640]{1,0:T(8,128)(2,1)S(1)}, bf16[128,640]{1,0:T(8,128)(2,1)}, u32[]{:S(2)}) copy-start(bf16[128,640]{1,0:T(8,128)(2,1)} %param.13) | copy-start | bytes 491524
Sparse Core Ops, SparseCore 0:
  11.3 100.9 all-gather.4
  116.2 75.1 all-gather.6
  194.6 93.1 all-gather.8
  294.1 87.4 all-reduce.1
where the time goes:
time: 392 us; the launch traced here: 390 us
  waiting for transfers between devices  207 us (53%)
  blocking collectives  99.6 us (25%)
  matrix products  23.8 us (6%)
  starting transfers between devices  16.7 us (4%)
  other arithmetic  15.4 us (4%)
  between operations  15.2 us (4%)
  local copies, waits for them, and re-layouts  11.5 us (3%)
    all_gather x1, blocking collectives, on_device(): segment_part = lax.all_gather(stretch_segments, 'seq', axis=0, tiled=True)  99.6 us
    all_gather x1, waiting for transfers between devices, on_device(): lax.all_gather(out_weight, 'seq', axis=1, tiled=True)  83.6 us
    psum x1, waiting for transfers between devices, on_device(): lax.psum(partial_value.astype(jnp.bfloat16), 'head').astype(jnp.float32)  82.9 us
    all_gather x1, waiting for transfers between devices, on_device(): value_part = lax.all_gather(block_value_rows, 'seq', axis=0, tiled=True)  39.6 us
    all_to_all x1, starting transfers between devices, on_device(): lax.all_to_all(outgoing, 'seq', split_axis=2, concat_axis=2, tiled=True)  16.6 us
    dot_general x1, matrix products, on_device(): jnp.einsum('kgtp,pkd->kgtd', weights.astype(jnp.bfloat16), value_three, p...  12.9 us
    unnamed x8, local copies, waits for them, and re-layouts  9.51 us
  transfers between devices with their start and end apart: 5, of which 3 were waited for; matrix products, arithmetic and copies ran while one was open for 11% of the time, Pallas kernels for 0%

commit v1 on v0

v1 whole, which is shorter than its diff:
```python
import functools

import jax
import jax.numpy as jnp
from jax import lax
from jax.experimental import pallas as pl
from jax.experimental.pallas import tpu as pltpu
from jax.sharding import PartitionSpec as P

HEAD_SIZE = 128
Z = 8
Y = 4
REQUESTS = 16
MESH = pl.DeviceIdType.MESH
KEY_BLOCKS = 8


def seq_id(z, y, c):
    return z * 8 + y * 2 + c


def meet(partners):
    barrier = pltpu.get_barrier_semaphore()
    for seq in partners:
        pl.semaphore_signal(barrier, inc=1, device_id={"seq": seq}, device_id_type=MESH)
    pl.semaphore_wait(barrier, len(partners))


def gather_kernel(kv_ref, w_ref, kv_all, w_all, send_sem, recv_sem, local_sem):
    me = lax.axis_index("seq")
    z, y, c = me // 8, (me // 2) % 4, me % 2
    rows = kv_ref.shape[0]
    cut = 144
    across = seq_id(z, y, 1 - c)
    up, down = seq_id((z + 1) % Z, y, c), seq_id((z + 7) % Z, y, c)
    meet([across, up, down] + [seq_id(z, (y + a) % Y, c) for a in (1, 2, 3)])

    used = [0]
    pending = []

    def send(src, dst, device):
        i = used[0]
        used[0] += 1
        copy = pltpu.make_async_remote_copy(
            src_ref=src,
            dst_ref=dst,
            send_sem=send_sem.at[i],
            recv_sem=recv_sem.at[i],
            device_id={"seq": device},
            device_id_type=MESH,
        )
        copy.start()
        pending.append(copy)
        return copy

    def kv_at(seq, part):
        lo, hi = part
        return kv_all.at[seq, pl.ds(lo, hi - lo)]

    whole = (0, rows)
    to_core = []
    own_kv = kv_all.at[me]
    ring = {}
    ring[0, 1, 1] = send(kv_ref, own_kv, up)
    ring[0, -1, 1] = send(kv_ref, own_kv, down)
    near = {}
    for a in (1, 3, 2):
        near[a] = send(kv_ref, own_kv, seq_id(z, (y + 4 - a) % Y, c))
    to_core.append(send(kv_ref, own_kv, across))
    near_w = {}
    w_slot = y * 2 + c
    for a in (1, 3, 2):
        near_w[a] = send(w_ref, w_all.at[w_slot], seq_id(z, (y + 4 - a) % Y, c))
    to_core.append(send(w_ref, w_all.at[w_slot], across))
    local = [
        pltpu.make_async_copy(kv_ref, own_kv, local_sem.at[0]),
        pltpu.make_async_copy(w_ref, w_all.at[w_slot], local_sem.at[1]),
    ]
    for copy in local:
        copy.start()

    def start_chain(a):
        seq = seq_id(z, (y + a) % Y, c)
        near[a].wait_recv()
        block = kv_at(seq, whole)
        ring[a, 1, 1] = send(block, block, up)
        ring[a, -1, 1] = send(block, block, down)
        to_core.append(send(block, block, across))

    def advance(a, k):
        for direction, target in ((1, up), (-1, down)):
            seq = seq_id((z + 8 - direction * k) % Z, (y + a) % Y, c)
            ring[a, direction, k].wait_recv()
            part = whole
            if k == 4:
                part = (0, cut) if direction == 1 else (cut, rows)
            block = kv_at(seq, part)
            if k < 4:
                onward = block
                if k == 3:
                    onward = kv_at(seq, (0, cut) if direction == 1 else (cut, rows))
                ring[a, direction, k + 1] = send(onward, onward, target)
            to_core.append(send(block, block, across))

    order = (0, 1, 3, 2)
    for tick in range(1, 9):
        for at, a in enumerate(order):
            k = tick - at
            if k == 0:
                start_chain(a)
            elif 1 <= k <= 4:
                advance(a, k)
    for a in (1, 3, 2):
        slot = (y + a) % Y * 2 + c
        near_w[a].wait_recv()
        to_core.append(send(w_all.at[slot], w_all.at[slot], across))
    for copy in to_core:
        copy.wait_recv()
    for copy in pending:
        copy.wait_send()
    for copy in local:
        copy.wait()


def gather_blocks(kv_block, w_block, seq_count):
    sems = 84
    return pl.pallas_call(
        gather_kernel,
        name="gather_blocks",
        out_shape=(
            jax.ShapeDtypeStruct((seq_count,) + kv_block.shape, kv_block.dtype),
            jax.ShapeDtypeStruct((2 * Y,) + w_block.shape, w_block.dtype),
        ),
        in_specs=[pl.BlockSpec(memory_space=pltpu.VMEM)] * 2,
        out_specs=[pl.BlockSpec(memory_space=pl.ANY)] * 2,
        scratch_shapes=[
            pltpu.SemaphoreType.DMA((sems,)),
            pltpu.SemaphoreType.DMA((sems,)),
            pltpu.SemaphoreType.DMA((2,)),
        ],
        compiler_params=pltpu.CompilerParams(collective_id=0, has_side_effects=True),
    )(kv_block, w_block)


def ring_kernel(x_ref, all_ref, send_sem, recv_sem, local_sem):
    me = lax.axis_index("seq")
    z, y, c = me // 8, (me // 2) % 4, me % 2
    rows = x_ref.shape[0]
    half = rows // 2
    up, down = seq_id((z + 1) % Z, y, c), seq_id((z + 7) % Z, y, c)
    meet([up, down])
    pending = []
    ring = {}

    def send(src, dst, device, direction, k):
        i = 2 * (k - 1) + (direction > 0)
        copy = pltpu.make_async_remote_copy(
            src_ref=src,
            dst_ref=dst,
            send_sem=send_sem.at[i],
            recv_sem=recv_sem.at[i],
            device_id={"seq": device},
            device_id_type=MESH,
        )
        copy.start()
        pending.append(copy)
        ring[direction, k] = copy

    send(x_ref, all_ref.at[z], up, 1, 1)
    send(x_ref, all_ref.at[z], down, -1, 1)
    local = pltpu.make_async_copy(x_ref, all_ref.at[z], local_sem)
    local.start()
    for k in (1, 2, 3, 4):
        for direction, target in ((1, up), (-1, down)):
            ring[direction, k].wait_recv()
            if k < 4:
                block = all_ref.at[(z + 8 - direction * k) % Z]
                if k == 3:
                    block = block.at[pl.ds(0, half)] if direction == 1 else block.at[pl.ds(half, half)]
                send(block, block, target, direction, k + 1)
    for copy in pending:
        copy.wait_send()
    local.wait()


def ring_gather(x):
    return pl.pallas_call(
        ring_kernel,
        name="ring_gather",
        out_shape=jax.ShapeDtypeStruct((Z,) + x.shape, x.dtype),
        in_specs=[pl.BlockSpec(memory_space=pltpu.VMEM)],
        out_specs=pl.BlockSpec(memory_space=pl.ANY),
        scratch_shapes=[
            pltpu.SemaphoreType.DMA((8,)),
            pltpu.SemaphoreType.DMA((8,)),
            pltpu.SemaphoreType.DMA,
        ],
        compiler_params=pltpu.CompilerParams(collective_id=1, has_side_effects=True),
    )(x)


def attention_kernel(q_ref, seg_ref, kv_ref, out_ref, qt_ref, top_ref, sum_ref, acc_ref):
    seq_place = lax.axis_index("seq")
    tokens = q_ref.shape[0]
    groups = q_ref.shape[1] // HEAD_SIZE
    span = KEY_BLOCKS * tokens
    factor = HEAD_SIZE ** (-0.5) * 1.4426950408889634
    table = jnp.sum(kv_ref[:, 2 * tokens :, :].astype(jnp.float32), axis=0)
    ids = lax.broadcasted_iota(jnp.int32, table.shape, 0)
    first = jnp.sum(jnp.where(ids == seg_ref[...], table, 0.0), axis=0, keepdims=True)
    lowest = jnp.min(first).astype(jnp.int32)
    highest = jnp.max(first).astype(jnp.int32)
    start = jnp.concatenate([first.astype(jnp.int32)] * groups, axis=1)
    place = lax.broadcasted_iota(jnp.int32, (1, tokens), 1) + seq_place * tokens
    place = jnp.concatenate([place] * groups, axis=1)
    for g in range(groups):
        qt_ref[g * tokens : (g + 1) * tokens, :] = q_ref[:, g * HEAD_SIZE : (g + 1) * HEAD_SIZE]
    top_ref[...] = jnp.full(top_ref.shape, -1e29, jnp.float32)
    sum_ref[...] = jnp.zeros(sum_ref.shape, jnp.float32)
    acc_ref[...] = jnp.zeros(acc_ref.shape, jnp.float32)

    def step(masked, i, carry):
        blocks = pl.ds(i * KEY_BLOCKS, KEY_BLOCKS)
        keys = kv_ref[blocks, 0:tokens, :].reshape(span, HEAD_SIZE)
        values = kv_ref[blocks, tokens : 2 * tokens, :].reshape(span, HEAD_SIZE)
        scores = lax.dot_general(
            keys, qt_ref[...], (((1,), (1,)), ((), ())), preferred_element_type=jnp.float32
        )
        if masked:
            key_place = lax.broadcasted_iota(jnp.int32, scores.shape, 0) + i * span
            allowed = (key_place >= start) & (key_place <= place)
            scores = jnp.where(allowed, scores, -1e30)
        old = top_ref[...]
        top = jnp.maximum(old, jnp.max(scores, axis=0, keepdims=True))
        weights = jnp.exp2((scores - top) * factor)
        shrink = jnp.exp2((old - top) * factor)
        top_ref[...] = top
        sum_ref[...] = sum_ref[...] * shrink + jnp.sum(weights, axis=0, keepdims=True)
        acc_ref[...] = acc_ref[...] * shrink + lax.dot_general(
            values,
            weights.astype(jnp.bfloat16),
            (((0,), (0,)), ((), ())),
            preferred_element_type=jnp.float32,
        )
        return carry

    begin = lowest // span
    end = (seq_place * tokens + tokens - 1) // span + 1
    clear_begin = jnp.minimum((highest + span - 1) // span, end)
    clear_end = jnp.maximum((seq_place * tokens + 1) // span, clear_begin)
    lax.fori_loop(begin, clear_begin, functools.partial(step, True), 0)
    lax.fori_loop(clear_begin, clear_end, functools.partial(step, False), 0)
    lax.fori_loop(clear_end, end, functools.partial(step, True), 0)
    result = acc_ref[...] / sum_ref[...]
    for g in range(groups):
        columns = slice(g * tokens, (g + 1) * tokens)
        out_ref[:, g * HEAD_SIZE : (g + 1) * HEAD_SIZE] = result[:, columns].T.astype(out_ref.dtype)


def attend(queries, segments, kv_all):
    tokens, width = queries.shape
    count = tokens * (width // HEAD_SIZE)
    return pl.pallas_call(
        attention_kernel,
        name="attend",
        out_shape=jax.ShapeDtypeStruct(queries.shape, queries.dtype),
        in_specs=[pl.BlockSpec(memory_space=pltpu.VMEM)] * 3,
        out_specs=pl.BlockSpec(memory_space=pltpu.VMEM),
        scratch_shapes=[
            pltpu.VMEM((count, HEAD_SIZE), jnp.bfloat16),
            pltpu.VMEM((1, count), jnp.float32),
            pltpu.VMEM((1, count), jnp.float32),
            pltpu.VMEM((HEAD_SIZE, count), jnp.float32),
        ],
    )(queries, segments, kv_all)


def on_device(
    block_query_rows,
    block_key_rows,
    block_value_rows,
    stretch_segments,
    residual,
    out_weight,
    cache_by_prefill,
    request_pages,
    request_owner,
):
    seq_count = lax.axis_size("seq")
    head_count = lax.axis_size("head")
    seq_place = lax.axis_index("seq")
    ids = jnp.arange(REQUESTS, dtype=jnp.int32)
    before = jnp.sum((stretch_segments[None, :] < ids[:, None]).astype(jnp.float32), axis=1)
    table = jnp.broadcast_to(before[:, None], (REQUESTS, HEAD_SIZE)).astype(jnp.bfloat16)
    kv_block = jnp.concatenate([block_key_rows, block_value_rows, table], axis=0)
    kv_all, w_all = gather_blocks(kv_block, out_weight.T, seq_count)
    attention = attend(block_query_rows, stretch_segments[None, :], kv_all)
    attention_all = ring_gather(attention)
    rows, width = attention.shape
    partial_sums = lax.dot_general(
        attention_all.reshape(Z * rows, width),
        w_all.reshape(width, width),
        (((1,), (1,)), ((), ())),
        preferred_element_type=jnp.float32,
    ).astype(jnp.bfloat16)
    parts = lax.all_to_all(
        partial_sums.reshape(Z, rows, width), "head", split_axis=0, concat_axis=0, tiled=True
    )
    total = jnp.sum(parts.astype(jnp.float32), axis=0).astype(jnp.bfloat16)
    pairs = [
        ((z * 8 + rest) * head_count + h, (h * 8 + rest) * head_count + z)
        for z in range(Z)
        for rest in range(8)
        for h in range(head_count)
    ]
    mine = lax.ppermute(total, ("seq", "head"), pairs)
    layer_out = (residual.astype(jnp.float32) + mine.astype(jnp.float32)).astype(jnp.bfloat16)
    local_pages = cache_by_prefill.shape[2]
    capacity = 2 * local_pages
    per_pair = capacity // seq_count
    owners = jnp.arange(seq_count, dtype=jnp.int32)
    run_pages = jnp.sum(
        jnp.where(request_owner[None, :] == owners[:, None], request_pages[None, :], 0), axis=1
    )
    run_start = jnp.sum(
        jnp.where(request_owner[None, :] < owners[:, None], request_pages[None, :], 0), axis=1
    )
    pair_slots = jnp.arange(per_pair, dtype=jnp.int32)
    offset = (seq_place - run_start) % seq_count
    slot_index = pair_slots[None, :] * seq_count + offset[:, None]
    sending = slot_index < run_pages[:, None]
    local_index = pair_slots[None, :] + ((run_start + offset - seq_place) // seq_count)[:, None]
    local_index = jnp.where(sending, local_index, 0).reshape(-1)
    picked = jnp.take(cache_by_prefill, local_index, axis=2)
    outgoing = jnp.where(
        sending.reshape(-1)[None, None, :, None, None], picked, jnp.zeros_like(picked)
    )
    incoming = lax.all_to_all(outgoing, "seq", split_axis=2, concat_axis=2, tiled=True)
    layers, pair_kv, _, page_len, width = incoming.shape
    arranged = jnp.swapaxes(
        incoming.reshape(layers, pair_kv, seq_count, per_pair, page_len, width), 2, 3
    )
    my_start = run_start[seq_place]
    my_pages = run_pages[seq_place]
    rotated = jnp.roll(arranged, -my_start, axis=3).reshape(
        layers, pair_kv, capacity, page_len, width
    )
    keep = jnp.arange(capacity, dtype=jnp.int32) < my_pages
    cache_decode = jnp.where(keep[None, None, :, None, None], rotated, jnp.zeros_like(rotated))
    return (layer_out, cache_decode)


def solution(mesh):
    return jax.shard_map(
        on_device,
        mesh=mesh,
        in_specs=(
            P("seq", "head"),
            P("seq", "head"),
            P("seq", "head"),
            P("seq"),
            P("seq", "head"),
            P("head", "seq"),
            P(None, None, "seq", None, "head"),
            P(),
            P(),
        ),
        out_specs=(P("seq", "head"), P(None, None, "seq", None, "head")),
        check_vma=False,
    )
```

time: 392 us -> 163 us (0.42)
  waiting for transfers between devices: 207 us -> 39.2 us
  blocking collectives: 99.6 us -> 0 us
  Pallas kernels: 0 us -> 90.4 us
  matrix products: 23.8 us -> 3.73 us
  between operations: 15.2 us -> 2.03 us
  local copies, waits for them, and re-layouts: 11.5 us -> 2.03 us
  other arithmetic: 15.4 us -> 6.77 us
    all_gather x3 -> x0, waiting for transfers between devices: 123 us -> none  [the longest x1 83.6 us: on_device(): lax.all_gather(out_weight, 'seq', axis=1, tiled=True)]
    all_gather x1 -> x0, blocking collectives: 99.6 us -> none  [on_device(): segment_part = lax.all_gather(stretch_segments, 'seq', axis=0, tiled=True)]
    pallas_call x0 -> x3, Pallas kernels: none -> 90.4 us  [the longest x1 51.6 us: gather_blocks(): pl.pallas_call(gather_kernel, name='gather_blocks', out_shape=(jax.ShapeD...]
    psum x1 -> x0, waiting for transfers between devices: 82.9 us -> none  [on_device(): lax.psum(partial_value.astype(jnp.bfloat16), 'head').astype(jnp.float32)]
    all_to_all x1, waiting for transfers between devices: 0.01 us -> 27.2 us  [on_device(): lax.all_to_all(outgoing, 'seq', split_axis=2, concat_axis=2, tiled=True)]
    dot_general x3 -> x1, matrix products: 23.8 us -> 3.73 us  [on_device(): lax.dot_general(attention_all.reshape(Z * rows, width), w_all.reshape(wid...]
    all_to_all x0 -> x1, waiting for transfers between devices: none -> 11.3 us  [on_device(): lax.all_to_all(partial_sums.reshape(Z, rows, width), 'head', split_axis=0...]
    all_to_all x1, starting transfers between devices: 16.6 us -> 6.4 us  [on_device(): lax.all_to_all(outgoing, 'seq', split_axis=2, concat_axis=2, tiled=True)]
  transfers between devices with their start and end apart: 5 -> 3, of which waited for: 3 -> 3; matrix products, arithmetic and copies ran while one was open for 11% -> 4% of each run, Pallas kernels for 0% -> 0%
where the time goes in v1:
time: 163 us
  Pallas kernels  90.4 us (55%)
  waiting for transfers between devices  39.2 us (24%)
  starting transfers between devices  18.5 us (11%)
  other arithmetic  6.77 us (4%)
  matrix products  3.73 us (2%)
  local copies, waits for them, and re-layouts  2.03 us (1%)
  between operations  2.03 us (1%)
    pallas_call x1, Pallas kernels, gather_blocks(): pl.pallas_call(gather_kernel, name='gather_blocks', out_shape=(jax.ShapeD...  51.6 us
    pallas_call x1, Pallas kernels, ring_gather(): pl.pallas_call(ring_kernel, name='ring_gather', out_shape=jax.ShapeDtypeS...  33.8 us
    all_to_all x1, waiting for transfers between devices, on_device(): lax.all_to_all(outgoing, 'seq', split_axis=2, concat_axis=2, tiled=True)  27.2 us
    all_to_all x1, waiting for transfers between devices, on_device(): lax.all_to_all(partial_sums.reshape(Z, rows, width), 'head', split_axis=0...  11.3 us
    ppermute x1, starting transfers between devices, on_device(): mine = lax.ppermute(total, ('seq', 'head'), pairs)  7.19 us
    all_to_all x1, starting transfers between devices, on_device(): lax.all_to_all(outgoing, 'seq', split_axis=2, concat_axis=2, tiled=True)  6.4 us
    pallas_call x1, Pallas kernels, attend(): pl.pallas_call(attention_kernel, name='attend', out_shape=jax.ShapeDtypeS...  4.96 us
    all_to_all x1, starting transfers between devices, on_device(): lax.all_to_all(partial_sums.reshape(Z, rows, width), 'head', split_axis=0...  4.85 us
  transfers between devices with their start and end apart: 3, of which 3 were waited for; matrix products, arithmetic and copies ran while one was open for 4% of the time, Pallas kernels for 0%

profile of v1, /device:TPU:6, one launch (start us, length us, event | category | flops | bytes accessed | tf_op | source)
XLA Modules:
  0.0 162.6 jit_solution(1555374955423276259)
XLA Ops:
  0.6 0.0 copy-start
  0.6 0.8 convert_reduce_fusion
  1.5 1.5 maximum_maximum_fusion.kv_ref
  3.0 51.6 %gather_blocks.1 = (bf16[64,272,128]{2,1,0:T(8,128)(2,1)}, bf16[8,80,640]{2,1,0:T(8,128)(2,1)}) custom-call(bf16[272,128]{1,0:T(8,128)(2,1)} %maximum_maximum_fusion.kv_ref, bf16[80,640]{1,0:T(8,128)(2,1)} %bitcast.35), custom_call_target="tpu_custom_call" | custom-call | tf_op jit(solution)/shard_map/gather_blocks/pallas_call | solution.py:127
  54.6 5.0 %attend.1.x_ref = bf16[128,640]{1,0:T(8,128)(2,1)} custom-call(bf16[128,640]{1,0:T(8,128)(2,1)} %q_ref.1, s32[1,128]{1,0:T(1,128)} %bitcast.36, bf16[64,272,128]{2,1,0:T(8,128)(2,1)} %get-tuple-element.4.kv_ref), custom_call_target="tpu_custom_call" | custom-call | tf_op jit(solution)/shard_map/attend/pallas_call | solution.py:263
  59.6 33.8 %ring_gather.1 = bf16[8,128,640]{2,1,0:T(8,128)(2,1)} custom-call(bf16[128,640]{1,0:T(8,128)(2,1)} %attend.1.x_ref), custom_call_target="tpu_custom_call" | custom-call | tf_op jit(solution)/shard_map/ring_gather/pallas_call | solution.py:187
  93.4 0.0 copy-done.4
  93.4 3.7 %convolution_convert_fusion = bf16[1024,640]{1,0:T(8,128)(2,1)} fusion(bf16[1024,640]{1,0:T(8,128)(2,1)} %bitcast.34, bf16[640,640]{1,0:T(8,128)(2,1)S(1)} %bitcast.37), kind=kOutput, calls=%fused_computation.3 | convolution fusion | flops 839516160 | bytes 3440640 | tf_op jit(solution)/shard_map/dot_general | solution.py:300
  97.2 4.9 %all-to-all-start = ((bf16[8,128,640]{2,1,0:T(8,128)(2,1)}), bf16[8,128,640]{2,1,0:T(8,128)(2,1)S(1)}, u32[]{:S(2)}, u32[]{:S(2)}) async-start(bf16[8,128,640]{2,1,0:T(8,128)(2,1)} %bitcast.4), calls=%async_computation | async-start | bytes 2621440 | tf_op jit(solution)/shard_map/all_to_all | solution.py:306
  102.0 0.1 select_reduce_fusion.1
  102.2 0.8 gather_fusion
  103.0 1.2 select_bitcast_fusion
  104.2 11.3 %all-to-all-done = bf16[8,128,640]{2,1,0:T(8,128)(2,1)S(1)} async-done(((bf16[8,128,640]{2,1,0:T(8,128)(2,1)}), bf16[8,128,640]{2,1,0:T(8,128)(2,1)S(1)}, u32[]{:S(2)}, u32[]{:S(2)}) %all-to-all-start) | async-done | bytes 1310752 | tf_op jit(solution)/shard_map/all_to_all | solution.py:306
  115.5 6.4 %all-to-all-start.1 = ((bf16[2,2,64,16,128]{4,3,1,0,2:T(8,128)(2,1)}), bf16[2,2,64,16,128]{4,3,1,0,2:T(8,128)(2,1)S(1)}, u32[]{:S(2)}, u32[]{:S(2)}) async-start(bf16[2,2,64,16,128]{4,3,1,0,2:T(8,128)(2,1)} %select_bitcast_fusion), calls=%async_computation.1 | async-start | bytes 2097152 | tf_op jit(solution)/shard_map/all_to_all | solution.py:338
  121.9 0.6 dynamic_slice.10
  122.5 0.6 dynamic_slice.11
  124.4 0.7 iota_compare_fusion.3
  125.0 0.2 reduce_sum.44
  125.2 0.0 copy-start.1
  125.2 7.2 %collective-permute-start = (bf16[128,640]{1,0:T(8,128)(2,1)S(1)}, bf16[128,640]{1,0:T(8,128)(2,1)S(1)}, u32[]{:S(2)}, u32[]{:S(2)}) collective-permute-start(bf16[128,640]{1,0:T(8,128)(2,1)S(1)} %reduce_sum.44), channel_id=1, source_target_pairs={{0,0},{1,64},{2,128},{3,192},{4,256},{5,320},{6,384},{7,448},{8,8}... | collective-permute-start | bytes 491528 | tf_op jit(solution)/shard_map/ppermute | solution.py:316
  132.4 27.2 %all-to-all-done.1 = bf16[2,2,64,16,128]{4,3,1,0,2:T(8,128)(2,1)S(1)} async-done(((bf16[2,2,64,16,128]{4,3,1,0,2:T(8,128)(2,1)}), bf16[2,2,64,16,128]{4,3,1,0,2:T(8,128)(2,1)S(1)}, u32[]{:S(2)}, u32[]{:S(2)}) %all-to-all-start.1) | async-done | bytes 1048608 | tf_op jit(solution)/shard_map/all_to_all | solution.py:338
  159.6 1.5 bitcast_select_fusion
  161.1 0.7 collective-permute-done
  161.9 0.7 add_convert_fusion
  (11 shorter events, 0.1 us)
Async XLA Ops:
  0.6 101.6 %copy-start = (bf16[2,2,32,16,128]{4,3,2,1,0:T(8,128)(2,1)S(1)}, bf16[2,2,32,16,128]{4,3,2,1,0:T(8,128)(2,1)}, u32[]{:S(2)}) copy-start(bf16[2,2,32,16,128]{4,3,2,1,0:T(8,128)(2,1)} %param.15) | copy-start | bytes 1572868
  59.6 33.8 %copy-start.4 = (bf16[8,80,640]{2,1,0:T(8,128)(2,1)S(1)}, bf16[8,80,640]{2,1,0:T(8,128)(2,1)}, u32[]{:S(2)}) copy-start(bf16[8,80,640]{2,1,0:T(8,128)(2,1)} %get-tuple-element.5) | copy-start | bytes 2457604
  97.2 4.9 %copy-start.2 = (s32[128]{0:T(128)S(1)}, s32[128]{0:T(128)}, u32[]{:S(2)}) copy-start(s32[128]{0:T(128)} %param.16) | copy-start | bytes 1540
  97.2 4.9 %copy-start.3 = (s32[128]{0:T(128)S(1)}, s32[128]{0:T(128)}, u32[]{:S(2)}) copy-start(s32[128]{0:T(128)} %param.17) | copy-start | bytes 1540
  97.2 18.3 %all-to-all-start = ((bf16[8,128,640]{2,1,0:T(8,128)(2,1)}), bf16[8,128,640]{2,1,0:T(8,128)(2,1)S(1)}, u32[]{:S(2)}, u32[]{:S(2)}) async-start(bf16[8,128,640]{2,1,0:T(8,128)(2,1)} %bitcast.4), calls=%async_computation | async-start | bytes 2621440 | tf_op jit(solution)/shard_map/all_to_all | solution.py:306
  115.5 44.1 %all-to-all-start.1 = ((bf16[2,2,64,16,128]{4,3,1,0,2:T(8,128)(2,1)}), bf16[2,2,64,16,128]{4,3,1,0,2:T(8,128)(2,1)S(1)}, u32[]{:S(2)}, u32[]{:S(2)}) async-start(bf16[2,2,64,16,128]{4,3,1,0,2:T(8,128)(2,1)} %select_bitcast_fusion), calls=%async_computation.1 | async-start | bytes 2097152 | tf_op jit(solution)/shard_map/all_to_all | solution.py:338
  125.2 36.6 %copy-start.1 = (bf16[128,640]{1,0:T(8,128)(2,1)S(1)}, bf16[128,640]{1,0:T(8,128)(2,1)}, u32[]{:S(2)}) copy-start(bf16[128,640]{1,0:T(8,128)(2,1)} %param.13) | copy-start | bytes 491524
  125.2 36.6 %collective-permute-start = (bf16[128,640]{1,0:T(8,128)(2,1)S(1)}, bf16[128,640]{1,0:T(8,128)(2,1)S(1)}, u32[]{:S(2)}, u32[]{:S(2)}) collective-permute-start(bf16[128,640]{1,0:T(8,128)(2,1)S(1)} %reduce_sum.44), channel_id=1, source_target_pairs={{0,0},{1,64},{2,128},{3,192},{4,256},{5,320},{6,384},{7,448},{8,8}... | collective-permute-start | bytes 491528 | tf_op jit(solution)/shard_map/ppermute | solution.py:316

commit v2 on v1

--- a/solution.py
+++ b/solution.py
@@ -26,14 +26,20 @@
     pl.semaphore_wait(barrier, len(partners))
 
 
-def gather_kernel(kv_ref, w_ref, kv_all, w_all, send_sem, recv_sem, local_sem):
+def gather_kernel(
+    kv_ref, w_ref, page_ref, kv_all, w_all, page_out, by_z, by_y, send_sem, recv_sem, local_sem
+):
     me = lax.axis_index("seq")
     z, y, c = me // 8, (me // 2) % 4, me % 2
     rows = kv_ref.shape[0]
     cut = 144
     across = seq_id(z, y, 1 - c)
     up, down = seq_id((z + 1) % Z, y, c), seq_id((z + 7) % Z, y, c)
-    meet([across, up, down] + [seq_id(z, (y + a) % Y, c) for a in (1, 2, 3)])
+    meet(
+        [across]
+        + [seq_id((z + d) % Z, y, c) for d in range(1, Z)]
+        + [seq_id(z, (y + a) % Y, c) for a in (1, 2, 3)]
+    )
 
     used = [0]
     pending = []
@@ -67,14 +73,11 @@
     for a in (1, 3, 2):
         near[a] = send(kv_ref, own_kv, seq_id(z, (y + 4 - a) % Y, c))
     to_core.append(send(kv_ref, own_kv, across))
-    near_w = {}
     w_slot = y * 2 + c
-    for a in (1, 3, 2):
-        near_w[a] = send(w_ref, w_all.at[w_slot], seq_id(z, (y + 4 - a) % Y, c))
-    to_core.append(send(w_ref, w_all.at[w_slot], across))
     local = [
         pltpu.make_async_copy(kv_ref, own_kv, local_sem.at[0]),
         pltpu.make_async_copy(w_ref, w_all.at[w_slot], local_sem.at[1]),
+        pltpu.make_async_copy(page_ref.at[z, y], by_z.at[z, y], local_sem.at[2]),
     ]
     for copy in local:
         copy.start()
@@ -102,6 +105,39 @@
                 ring[a, direction, k + 1] = send(onward, onward, target)
             to_core.append(send(block, block, across))
 
+    page_z = {}
+    page_y = {}
+
+    def pages_over_z(d):
+        to = (z + d) % Z
+        page_z[d] = send(page_ref.at[to], by_z.at[z], seq_id(to, y, c))
+
+    def pages_over_y(d):
+        if d:
+            page_z[d].wait_recv()
+        source = (z + 8 - d) % Z
+        held = by_z if d else page_ref
+        for a in (1, 3, 2):
+            to = (y + a) % Y
+            page_y[d, a] = send(held.at[source, to], by_y.at[source, y], seq_id(z, to, c))
+
+    near_w = {}
+
+    def send_weight():
+        for a in (1, 3, 2):
+            near_w[a] = send(w_ref, w_all.at[w_slot], seq_id(z, (y + 4 - a) % Y, c))
+        to_core.append(send(w_ref, w_all.at[w_slot], across))
+
+    extra = {
+        1: [(pages_over_z, 4), (pages_over_y, 0)],
+        2: [(pages_over_z, 3), (pages_over_z, 5)],
+        3: [(pages_over_z, 2), (pages_over_z, 6)],
+        4: [(pages_over_z, 1), (pages_over_z, 7)],
+        5: [(pages_over_y, 4)],
+        6: [(pages_over_y, 3), (pages_over_y, 5)],
+        7: [(pages_over_y, 2), (pages_over_y, 6)],
+        8: [(pages_over_y, 1), (pages_over_y, 7)],
+    }
     order = (0, 1, 3, 2)
     for tick in range(1, 9):
         for at, a in enumerate(order):
@@ -110,6 +146,25 @@
                 start_chain(a)
             elif 1 <= k <= 4:
                 advance(a, k)
+        for action, d in extra[tick]:
+            action(d)
+        if tick == 4:
+            send_weight()
+    for copy in local:
+        copy.wait()
+    own_pages = []
+    for at, a in enumerate((0, 1, 3, 2)):
+        ys = (y + 4 - a) % Y
+        held = by_y if a else by_z
+        for d in range(Z):
+            if a:
+                page_y[d, a].wait_recv()
+        to_core.append(send(held.at[:, ys, 1 - c], page_out.at[:, ys, c], across))
+        copy = pltpu.make_async_copy(
+            held.at[:, ys, c], page_out.at[:, ys, c], local_sem.at[3 + at]
+        )
+        copy.start()
+        own_pages.append(copy)
     for a in (1, 3, 2):
         slot = (y + a) % Y * 2 + c
         near_w[a].wait_recv()
@@ -118,28 +173,32 @@
         copy.wait_recv()
     for copy in pending:
         copy.wait_send()
-    for copy in local:
+    for copy in own_pages:
         copy.wait()
 
 
-def gather_blocks(kv_block, w_block, seq_count):
-    sems = 84
+def gather_blocks(kv_block, w_block, pages, seq_count):
+    sems = 128
     return pl.pallas_call(
         gather_kernel,
         name="gather_blocks",
         out_shape=(
             jax.ShapeDtypeStruct((seq_count,) + kv_block.shape, kv_block.dtype),
             jax.ShapeDtypeStruct((2 * Y,) + w_block.shape, w_block.dtype),
+            jax.ShapeDtypeStruct(pages.shape, pages.dtype),
         ),
-        in_specs=[pl.BlockSpec(memory_space=pltpu.VMEM)] * 2,
-        out_specs=[pl.BlockSpec(memory_space=pl.ANY)] * 2,
+        in_specs=[pl.BlockSpec(memory_space=pltpu.VMEM)] * 3,
+        out_specs=[pl.BlockSpec(memory_space=pl.ANY)] * 2
+        + [pl.BlockSpec(memory_space=pltpu.VMEM)],
         scratch_shapes=[
+            pltpu.VMEM(pages.shape, pages.dtype),
+            pltpu.VMEM(pages.shape, pages.dtype),
             pltpu.SemaphoreType.DMA((sems,)),
             pltpu.SemaphoreType.DMA((sems,)),
-            pltpu.SemaphoreType.DMA((2,)),
+            pltpu.SemaphoreType.DMA((7,)),
         ],
         compiler_params=pltpu.CompilerParams(collective_id=0, has_side_effects=True),
-    )(kv_block, w_block)
+    )(kv_block, w_block, pages)
 
 
 def ring_kernel(x_ref, all_ref, send_sem, recv_sem, local_sem):
@@ -289,11 +348,35 @@
     seq_count = lax.axis_size("seq")
     head_count = lax.axis_size("head")
     seq_place = lax.axis_index("seq")
+    local_pages = cache_by_prefill.shape[2]
+    capacity = 2 * local_pages
+    per_pair = capacity // seq_count
+    owners = jnp.arange(seq_count, dtype=jnp.int32)
+    run_pages = jnp.sum(
+        jnp.where(request_owner[None, :] == owners[:, None], request_pages[None, :], 0), axis=1
+    )
+    run_start = jnp.sum(
+        jnp.where(request_owner[None, :] < owners[:, None], request_pages[None, :], 0), axis=1
+    )
+    pair_slots = jnp.arange(per_pair, dtype=jnp.int32)
+    offset = (seq_place - run_start) % seq_count
+    slot_index = pair_slots[None, :] * seq_count + offset[:, None]
+    sending = slot_index < run_pages[:, None]
+    local_index = pair_slots[None, :] + ((run_start + offset - seq_place) // seq_count)[:, None]
+    local_index = jnp.where(sending, local_index, 0).reshape(-1)
+    picked = jnp.take(cache_by_prefill, local_index, axis=2)
+    outgoing = jnp.where(
+        sending.reshape(-1)[None, None, :, None, None], picked, jnp.zeros_like(picked)
+    )
+    pages = jnp.moveaxis(outgoing, 2, 0)
     ids = jnp.arange(REQUESTS, dtype=jnp.int32)
     before = jnp.sum((stretch_segments[None, :] < ids[:, None]).astype(jnp.float32), axis=1)
     table = jnp.broadcast_to(before[:, None], (REQUESTS, HEAD_SIZE)).astype(jnp.bfloat16)
     kv_block = jnp.concatenate([block_key_rows, block_value_rows, table], axis=0)
-    kv_all, w_all = gather_blocks(kv_block, out_weight.T, seq_count)
+    kv_all, w_all, moved = gather_blocks(
+        kv_block, out_weight.T, pages.reshape(Z, Y, 2, -1, HEAD_SIZE), seq_count
+    )
+    incoming = jnp.moveaxis(moved.reshape(pages.shape), 0, 2)
     attention = attend(block_query_rows, stretch_segments[None, :], kv_all)
     attention_all = ring_gather(attention)
     rows, width = attention.shape
@@ -315,27 +398,6 @@
     ]
     mine = lax.ppermute(total, ("seq", "head"), pairs)
     layer_out = (residual.astype(jnp.float32) + mine.astype(jnp.float32)).astype(jnp.bfloat16)
-    local_pages = cache_by_prefill.shape[2]
-    capacity = 2 * local_pages
-    per_pair = capacity // seq_count
-    owners = jnp.arange(seq_count, dtype=jnp.int32)
-    run_pages = jnp.sum(
-        jnp.where(request_owner[None, :] == owners[:, None], request_pages[None, :], 0), axis=1
-    )
-    run_start = jnp.sum(
-        jnp.where(request_owner[None, :] < owners[:, None], request_pages[None, :], 0), axis=1
-    )
-    pair_slots = jnp.arange(per_pair, dtype=jnp.int32)
-    offset = (seq_place - run_start) % seq_count
-    slot_index = pair_slots[None, :] * seq_count + offset[:, None]
-    sending = slot_index < run_pages[:, None]
-    local_index = pair_slots[None, :] + ((run_start + offset - seq_place) // seq_count)[:, None]
-    local_index = jnp.where(sending, local_index, 0).reshape(-1)
-    picked = jnp.take(cache_by_prefill, local_index, axis=2)
-    outgoing = jnp.where(
-        sending.reshape(-1)[None, None, :, None, None], picked, jnp.zeros_like(picked)
-    )
-    incoming = lax.all_to_all(outgoing, "seq", split_axis=2, concat_axis=2, tiled=True)
     layers, pair_kv, _, page_len, width = incoming.shape
     arranged = jnp.swapaxes(
         incoming.reshape(layers, pair_kv, seq_count, per_pair, page_len, width), 2, 3

time: 163 us -> 169 us (1.037)
  Pallas kernels: 90.4 us -> 124 us
  waiting for transfers between devices: 39.2 us -> 19.7 us
  starting transfers between devices: 18.5 us -> 9.92 us
    pallas_call x1, Pallas kernels: 51.6 us -> 88.3 us  [gather_blocks(): pl.pallas_call(gather_kernel, name='gather_blocks', out_shape=(jax.ShapeD...]
    all_to_all x1 -> x0, waiting for transfers between devices: 27.2 us -> none  [on_device(): lax.all_to_all(outgoing, 'seq', split_axis=2, concat_axis=2, tiled=True)]
    ppermute x1, waiting for transfers between devices: 0.73 us -> 8.42 us  [on_device(): mine = lax.ppermute(total, ('seq', 'head'), pairs)]
    all_to_all x1 -> x0, starting transfers between devices: 6.4 us -> none  [on_device(): lax.all_to_all(outgoing, 'seq', split_axis=2, concat_axis=2, tiled=True)]
    pallas_call x1, Pallas kernels: 33.8 us -> 31.2 us  [ring_gather(): pl.pallas_call(ring_kernel, name='ring_gather', out_shape=jax.ShapeDtypeS...]
    ppermute x1, starting transfers between devices: 7.19 us -> 5.16 us  [on_device(): mine = lax.ppermute(total, ('seq', 'head'), pairs)]
  transfers between devices with their start and end apart: 3 -> 2, of which waited for: 3 -> 2; matrix products, arithmetic and copies ran while one was open for 4% -> 2% of each run, Pallas kernels for 0% -> 0%
where the time goes in v2:
time: 169 us
  Pallas kernels  124 us (73%)
  waiting for transfers between devices  19.7 us (12%)
  starting transfers between devices  9.92 us (6%)
  other arithmetic  6.66 us (4%)
  matrix products  3.74 us (2%)
  between operations  2.09 us (1%)
  local copies, waits for them, and re-layouts  2 us (1%)
    pallas_call x1, Pallas kernels, gather_blocks(): pl.pallas_call(gather_kernel, name='gather_blocks', out_shape=(jax.ShapeD...  88.3 us
    pallas_call x1, Pallas kernels, ring_gather(): pl.pallas_call(ring_kernel, name='ring_gather', out_shape=jax.ShapeDtypeS...  31.2 us
    all_to_all x1, waiting for transfers between devices, on_device(): lax.all_to_all(partial_sums.reshape(Z, rows, width), 'head', split_axis=0...  11.3 us
    ppermute x1, waiting for transfers between devices, on_device(): mine = lax.ppermute(total, ('seq', 'head'), pairs)  8.42 us
    ppermute x1, starting transfers between devices, on_device(): mine = lax.ppermute(total, ('seq', 'head'), pairs)  5.16 us
    pallas_call x1, Pallas kernels, attend(): pl.pallas_call(attention_kernel, name='attend', out_shape=jax.ShapeDtypeS...  4.95 us
    all_to_all x1, starting transfers between devices, on_device(): lax.all_to_all(partial_sums.reshape(Z, rows, width), 'head', split_axis=0...  4.76 us
    dot_general x1, matrix products, on_device(): lax.dot_general(attention_all.reshape(Z * rows, width), w_all.reshape(wid...  3.74 us
  transfers between devices with their start and end apart: 2, of which 2 were waited for; matrix products, arithmetic and copies ran while one was open for 2% of the time, Pallas kernels for 0%

profile of v2, /device:TPU:6, one launch (start us, length us, event | category | flops | bytes accessed | tf_op | source)
XLA Modules:
  0.0 168.6 jit_solution(10313307852892432017)
XLA Ops:
  0.6 0.0 copy-start
  0.7 0.8 select_reduce_fusion.1
  1.6 0.8 convert_reduce_fusion
  2.4 0.8 gather_fusion
  3.2 0.0 copy-done.3
  3.2 0.0 copy-done.4
  3.2 0.7 maximum_maximum_fusion.kv_ref
  3.9 1.2 select_select_fusion
  5.1 88.3 %gather_blocks.1 = (bf16[64,272,128]{2,1,0:T(8,128)(2,1)}, bf16[8,80,640]{2,1,0:T(8,128)(2,1)}, bf16[8,4,2,64,128]{4,3,2,1,0:T(8,128)(2,1)}) custom-call(bf16[272,128]{1,0:T(8,128)(2,1)} %maximum_maximum_fusion.kv_ref, bf16[80,640]{1,0:T(8,128)(2,1)} %bitcast.39, bf16[8,4,2,64,128]{4,3,2,1,0:T(8,128)(2,1)} %bitcast.36), custom_call_target="tpu_custom_call" | custom-call | tf_op jit(solution)/shard_map/gather_blocks/pallas_call | solution.py:182
  93.4 5.0 %attend.1.x_ref = bf16[128,640]{1,0:T(8,128)(2,1)} custom-call(bf16[128,640]{1,0:T(8,128)(2,1)} %q_ref.1, s32[1,128]{1,0:T(1,128)} %bitcast.40, bf16[64,272,128]{2,1,0:T(8,128)(2,1)} %get-tuple-element.5.kv_ref), custom_call_target="tpu_custom_call" | custom-call | tf_op jit(solution)/shard_map/attend/pallas_call | solution.py:322
  98.4 31.2 %ring_gather.1 = bf16[8,128,640]{2,1,0:T(8,128)(2,1)} custom-call(bf16[128,640]{1,0:T(8,128)(2,1)} %attend.1.x_ref), custom_call_target="tpu_custom_call" | custom-call | tf_op jit(solution)/shard_map/ring_gather/pallas_call | solution.py:246
  129.6 3.7 %convolution_convert_fusion = bf16[1024,640]{1,0:T(8,128)(2,1)} fusion(bf16[1024,640]{1,0:T(8,128)(2,1)} %bitcast.37, bf16[640,640]{1,0:T(8,128)(2,1)S(1)} %bitcast.41), kind=kOutput, calls=%fused_computation.3 | convolution fusion | flops 839516160 | bytes 3440640 | tf_op jit(solution)/shard_map/dot_general | solution.py:383
  133.3 4.8 %all-to-all-start = ((bf16[8,128,640]{2,1,0:T(8,128)(2,1)}), bf16[8,128,640]{2,1,0:T(8,128)(2,1)S(1)}, u32[]{:S(2)}, u32[]{:S(2)}) async-start(bf16[8,128,640]{2,1,0:T(8,128)(2,1)} %bitcast.8), calls=%async_computation | async-start | bytes 2621440 | tf_op jit(solution)/shard_map/all_to_all | solution.py:389
  138.1 0.6 dynamic_slice.10
  138.7 0.6 dynamic_slice.11
  140.6 0.7 iota_compare_fusion.3
  141.2 11.3 %all-to-all-done = bf16[8,128,640]{2,1,0:T(8,128)(2,1)S(1)} async-done(((bf16[8,128,640]{2,1,0:T(8,128)(2,1)}), bf16[8,128,640]{2,1,0:T(8,128)(2,1)S(1)}, u32[]{:S(2)}, u32[]{:S(2)}) %all-to-all-start) | async-done | bytes 1310752 | tf_op jit(solution)/shard_map/all_to_all | solution.py:389
  152.5 0.2 reduce_sum.48
  152.7 0.0 copy-start.2
  152.7 5.2 %collective-permute-start = (bf16[128,640]{1,0:T(8,128)(2,1)S(1)}, bf16[128,640]{1,0:T(8,128)(2,1)S(1)}, u32[]{:S(2)}, u32[]{:S(2)}) collective-permute-start(bf16[128,640]{1,0:T(8,128)(2,1)S(1)} %reduce_sum.48), channel_id=1, source_target_pairs={{0,0},{1,64},{2,128},{3,192},{4,256},{5,320},{6,384},{7,448},{8,8}... | collective-permute-start | bytes 491528 | tf_op jit(solution)/shard_map/ppermute | solution.py:399
  157.9 1.5 bitcast_select_fusion
  159.4 8.4 %collective-permute-done = bf16[128,640]{1,0:T(8,128)(2,1)S(1)} collective-permute-done((bf16[128,640]{1,0:T(8,128)(2,1)S(1)}, bf16[128,640]{1,0:T(8,128)(2,1)S(1)}, u32[]{:S(2)}, u32[]{:S(2)}) %collective-permute-start) | collective-permute-done | bytes 163872 | tf_op jit(solution)/shard_map/ppermute | solution.py:399
  167.8 0.0 copy-done.2
  167.9 0.7 add_convert_fusion
  (11 shorter events, 0.1 us)
Async XLA Ops:
  0.6 1.7 %copy-start = (bf16[2,2,32,16,128]{4,3,2,1,0:T(8,128)(2,1)S(1)}, bf16[2,2,32,16,128]{4,3,2,1,0:T(8,128)(2,1)}, u32[]{:S(2)}) copy-start(bf16[2,2,32,16,128]{4,3,2,1,0:T(8,128)(2,1)} %param.15) | copy-start | bytes 1572868
  0.6 2.5 %copy-start.3 = (bf16[128,128]{1,0:T(8,128)(2,1)S(1)}, bf16[128,128]{1,0:T(8,128)(2,1)}, u32[]{:S(2)}) copy-start(bf16[128,128]{1,0:T(8,128)(2,1)} %param.11) | copy-start | bytes 98308
  0.7 2.5 %copy-start.4 = (bf16[128,128]{1,0:T(8,128)(2,1)S(1)}, bf16[128,128]{1,0:T(8,128)(2,1)}, u32[]{:S(2)}) copy-start(bf16[128,128]{1,0:T(8,128)(2,1)} %param.10) | copy-start | bytes 98308
  98.4 31.2 %copy-start.5 = (bf16[8,80,640]{2,1,0:T(8,128)(2,1)S(1)}, bf16[8,80,640]{2,1,0:T(8,128)(2,1)}, u32[]{:S(2)}) copy-start(bf16[8,80,640]{2,1,0:T(8,128)(2,1)} %get-tuple-element.6) | copy-start | bytes 2457604
  133.3 19.2 %all-to-all-start = ((bf16[8,128,640]{2,1,0:T(8,128)(2,1)}), bf16[8,128,640]{2,1,0:T(8,128)(2,1)S(1)}, u32[]{:S(2)}, u32[]{:S(2)}) async-start(bf16[8,128,640]{2,1,0:T(8,128)(2,1)} %bitcast.8), calls=%async_computation | async-start | bytes 2621440 | tf_op jit(solution)/shard_map/all_to_all | solution.py:389
  138.1 19.8 %copy-start.1 = (bf16[8,4,2,64,128]{4,3,2,1,0:T(8,128)(2,1)S(1)}, bf16[8,4,2,64,128]{4,3,2,1,0:T(8,128)(2,1)}, u32[]{:S(2)}) copy-start(bf16[8,4,2,64,128]{4,3,2,1,0:T(8,128)(2,1)} %get-tuple-element.7) | copy-start | bytes 3145732
  152.7 15.1 %copy-start.2 = (bf16[128,640]{1,0:T(8,128)(2,1)S(1)}, bf16[128,640]{1,0:T(8,128)(2,1)}, u32[]{:S(2)}) copy-start(bf16[128,640]{1,0:T(8,128)(2,1)} %param.13) | copy-start | bytes 491524
  152.7 15.1 %collective-permute-start = (bf16[128,640]{1,0:T(8,128)(2,1)S(1)}, bf16[128,640]{1,0:T(8,128)(2,1)S(1)}, u32[]{:S(2)}, u32[]{:S(2)}) collective-permute-start(bf16[128,640]{1,0:T(8,128)(2,1)S(1)} %reduce_sum.48), channel_id=1, source_target_pairs={{0,0},{1,64},{2,128},{3,192},{4,256},{5,320},{6,384},{7,448},{8,8}... | collective-permute-start | bytes 491528 | tf_op jit(solution)/shard_map/ppermute | solution.py:399

commit v3 on v1

--- a/solution.py
+++ b/solution.py
@@ -33,7 +33,7 @@
     cut = 144
     across = seq_id(z, y, 1 - c)
     up, down = seq_id((z + 1) % Z, y, c), seq_id((z + 7) % Z, y, c)
-    meet([across, up, down] + [seq_id(z, (y + a) % Y, c) for a in (1, 2, 3)])
+    meet([across, up, down] + [seq_id(z, (y + a) % Y, c) for a in (1, 3)])
 
     used = [0]
     pending = []
@@ -64,14 +64,12 @@
     ring[0, 1, 1] = send(kv_ref, own_kv, up)
     ring[0, -1, 1] = send(kv_ref, own_kv, down)
     near = {}
-    for a in (1, 3, 2):
-        near[a] = send(kv_ref, own_kv, seq_id(z, (y + 4 - a) % Y, c))
+    left, right = seq_id(z, (y + 3) % Y, c), seq_id(z, (y + 1) % Y, c)
+    near[1] = [send(kv_ref, own_kv, left)]
+    near[3] = [send(kv_ref, own_kv, right)]
+    near[2] = []
     to_core.append(send(kv_ref, own_kv, across))
-    near_w = {}
     w_slot = y * 2 + c
-    for a in (1, 3, 2):
-        near_w[a] = send(w_ref, w_all.at[w_slot], seq_id(z, (y + 4 - a) % Y, c))
-    to_core.append(send(w_ref, w_all.at[w_slot], across))
     local = [
         pltpu.make_async_copy(kv_ref, own_kv, local_sem.at[0]),
         pltpu.make_async_copy(w_ref, w_all.at[w_slot], local_sem.at[1]),
@@ -81,8 +79,15 @@
 
     def start_chain(a):
         seq = seq_id(z, (y + a) % Y, c)
-        near[a].wait_recv()
+        for copy in near[a]:
+            copy.wait_recv()
         block = kv_at(seq, whole)
+        if a == 1:
+            half = kv_at(seq, (0, cut))
+            near[2].append(send(half, half, left))
+        if a == 3:
+            half = kv_at(seq, (cut, rows))
+            near[2].append(send(half, half, right))
         ring[a, 1, 1] = send(block, block, up)
         ring[a, -1, 1] = send(block, block, down)
         to_core.append(send(block, block, across))
@@ -102,18 +107,41 @@
                 ring[a, direction, k + 1] = send(onward, onward, target)
             to_core.append(send(block, block, across))
 
-    order = (0, 1, 3, 2)
-    for tick in range(1, 9):
-        for at, a in enumerate(order):
-            k = tick - at
+    near_w = {2: []}
+
+    def send_weight():
+        mine = w_all.at[w_slot]
+        near_w[1] = [send(w_ref, mine, left)]
+        near_w[3] = [send(w_ref, mine, right)]
+        to_core.append(send(w_ref, mine, across))
+
+    def weight_from(a):
+        slot = (y + a) % Y * 2 + c
+        block = w_all.at[slot]
+        for copy in near_w[a]:
+            copy.wait_recv()
+        if a == 1:
+            half = block.at[pl.ds(0, 48)]
+            near_w[2].append(send(half, half, left))
+        if a == 3:
+            half = block.at[pl.ds(48, 32)]
+            near_w[2].append(send(half, half, right))
+        to_core.append(send(block, block, across))
+
+    delay = {0: 0, 1: 1, 3: 1, 2: 3}
+    for tick in range(1, 8):
+        for a, late in delay.items():
+            k = tick - late
             if k == 0:
                 start_chain(a)
             elif 1 <= k <= 4:
                 advance(a, k)
-    for a in (1, 3, 2):
-        slot = (y + a) % Y * 2 + c
-        near_w[a].wait_recv()
-        to_core.append(send(w_all.at[slot], w_all.at[slot], across))
+        if tick == 1:
+            send_weight()
+        if tick == 4:
+            weight_from(1)
+            weight_from(3)
+    weight_from(2)
     for copy in to_core:
         copy.wait_recv()
     for copy in pending:
@@ -272,6 +300,7 @@
             pltpu.VMEM((1, count), jnp.float32),
             pltpu.VMEM((HEAD_SIZE, count), jnp.float32),
         ],
+        cost_estimate=pl.CostEstimate(flops=0, bytes_accessed=100_000_000, transcendentals=0),
     )(queries, segments, kv_all)
 
 
@@ -294,8 +323,31 @@
     table = jnp.broadcast_to(before[:, None], (REQUESTS, HEAD_SIZE)).astype(jnp.bfloat16)
     kv_block = jnp.concatenate([block_key_rows, block_value_rows, table], axis=0)
     kv_all, w_all = gather_blocks(kv_block, out_weight.T, seq_count)
+    local_pages = cache_by_prefill.shape[2]
+    capacity = 2 * local_pages
+    per_pair = capacity // seq_count
+    owners = jnp.arange(seq_count, dtype=jnp.int32)
+    run_pages = jnp.sum(
+        jnp.where(request_owner[None, :] == owners[:, None], request_pages[None, :], 0), axis=1
+    )
+    run_start = jnp.sum(
+        jnp.where(request_owner[None, :] < owners[:, None], request_pages[None, :], 0), axis=1
+    )
+    pair_slots = jnp.arange(per_pair, dtype=jnp.int32)
+    offset = (seq_place - run_start) % seq_count
+    slot_index = pair_slots[None, :] * seq_count + offset[:, None]
+    sending = slot_index < run_pages[:, None]
+    local_index = pair_slots[None, :] + ((run_start + offset - seq_place) // seq_count)[:, None]
+    local_index = jnp.where(sending, local_index, 0).reshape(-1)
+    picked = jnp.take(cache_by_prefill, local_index, axis=2)
+    outgoing = jnp.where(
+        sending.reshape(-1)[None, None, :, None, None], picked, jnp.zeros_like(picked)
+    )
+    outgoing, kv_all = lax.optimization_barrier((outgoing, kv_all))
+    incoming = lax.all_to_all(outgoing, "seq", split_axis=2, concat_axis=2, tiled=True)
     attention = attend(block_query_rows, stretch_segments[None, :], kv_all)
     attention_all = ring_gather(attention)
+    attention_all, incoming = lax.optimization_barrier((attention_all, incoming))
     rows, width = attention.shape
     partial_sums = lax.dot_general(
         attention_all.reshape(Z * rows, width),
@@ -315,27 +367,6 @@
     ]
     mine = lax.ppermute(total, ("seq", "head"), pairs)
     layer_out = (residual.astype(jnp.float32) + mine.astype(jnp.float32)).astype(jnp.bfloat16)
-    local_pages = cache_by_prefill.shape[2]
-    capacity = 2 * local_pages
-    per_pair = capacity // seq_count
-    owners = jnp.arange(seq_count, dtype=jnp.int32)
-    run_pages = jnp.sum(
-        jnp.where(request_owner[None, :] == owners[:, None], request_pages[None, :], 0), axis=1
-    )
-    run_start = jnp.sum(
-        jnp.where(request_owner[None, :] < owners[:, None], request_pages[None, :], 0), axis=1
-    )
-    pair_slots = jnp.arange(per_pair, dtype=jnp.int32)
-    offset = (seq_place - run_start) % seq_count
-    slot_index = pair_slots[None, :] * seq_count + offset[:, None]
-    sending = slot_index < run_pages[:, None]
-    local_index = pair_slots[None, :] + ((run_start + offset - seq_place) // seq_count)[:, None]
-    local_index = jnp.where(sending, local_index, 0).reshape(-1)
-    picked = jnp.take(cache_by_prefill, local_index, axis=2)
-    outgoing = jnp.where(
-        sending.reshape(-1)[None, None, :, None, None], picked, jnp.zeros_like(picked)
-    )
-    incoming = lax.all_to_all(outgoing, "seq", split_axis=2, concat_axis=2, tiled=True)
     layers, pair_kv, _, page_len, width = incoming.shape
     arranged = jnp.swapaxes(
         incoming.reshape(layers, pair_kv, seq_count, per_pair, page_len, width), 2, 3

time: 163 us -> 153 us (0.939)
  waiting for transfers between devices: 39.2 us -> 19.2 us
  Pallas kernels: 90.4 us -> 101 us
    all_to_all x1, waiting for transfers between devices: 27.2 us -> 0.01 us  [on_device(): lax.all_to_all(outgoing, 'seq', split_axis=2, concat_axis=2, tiled=True)]
    pallas_call x1, Pallas kernels: 33.8 us -> 47.7 us  [ring_gather(): pl.pallas_call(ring_kernel, name='ring_gather', out_shape=jax.ShapeDtypeS...]
    ppermute x1, waiting for transfers between devices: 0.73 us -> 7.98 us  [on_device(): mine = lax.ppermute(total, ('seq', 'head'), pairs)]
    pallas_call x1, Pallas kernels: 51.6 us -> 48.5 us  [gather_blocks(): pl.pallas_call(gather_kernel, name='gather_blocks', out_shape=(jax.ShapeD...]
  transfers between devices with their start and end apart: 3 -> 3, of which waited for: 3 -> 2; matrix products, arithmetic and copies ran while one was open for 4% -> 2% of each run, Pallas kernels for 0% -> 34%
where the time goes in v3:
time: 153 us
  Pallas kernels  101 us (66%)
  waiting for transfers between devices  19.2 us (13%)
  starting transfers between devices  18.3 us (12%)
  other arithmetic  6.66 us (4%)
  matrix products  3.74 us (2%)
  between operations  2.09 us (1%)
  local copies, waits for them, and re-layouts  2 us (1%)
    pallas_call x1, Pallas kernels, gather_blocks(): pl.pallas_call(gather_kernel, name='gather_blocks', out_shape=(jax.ShapeD...  48.5 us
    pallas_call x1, Pallas kernels, ring_gather(): pl.pallas_call(ring_kernel, name='ring_gather', out_shape=jax.ShapeDtypeS...  47.7 us
    all_to_all x1, waiting for transfers between devices, on_device(): lax.all_to_all(partial_sums.reshape(Z, rows, width), 'head', split_axis=0...  11.3 us
    ppermute x1, waiting for transfers between devices, on_device(): mine = lax.ppermute(total, ('seq', 'head'), pairs)  7.98 us
    all_to_all x1, starting transfers between devices, on_device(): lax.all_to_all(outgoing, 'seq', split_axis=2, concat_axis=2, tiled=True)  7.96 us
    ppermute x1, starting transfers between devices, on_device(): mine = lax.ppermute(total, ('seq', 'head'), pairs)  5.58 us
    pallas_call x1, Pallas kernels, attend(): pl.pallas_call(attention_kernel, name='attend', out_shape=jax.ShapeDtypeS...  4.95 us
    all_to_all x1, starting transfers between devices, on_device(): lax.all_to_all(partial_sums.reshape(Z, rows, width), 'head', split_axis=0...  4.77 us
  transfers between devices with their start and end apart: 3, of which 2 were waited for; matrix products, arithmetic and copies ran while one was open for 2% of the time, Pallas kernels for 34%

profile of v3, /device:TPU:6, one launch (start us, length us, event | category | flops | bytes accessed | tf_op | source)
XLA Modules:
  0.0 153.2 jit_solution(9434526381476359263)
XLA Ops:
  0.6 0.0 copy-start
  0.7 0.8 select_reduce_fusion.1
  1.6 0.8 convert_reduce_fusion
  2.4 0.0 copy-done
  2.4 0.8 gather_fusion
  3.2 0.7 maximum_maximum_fusion.kv_ref
  3.9 48.5 %gather_blocks.1 = (bf16[64,272,128]{2,1,0:T(8,128)(2,1)}, bf16[8,80,640]{2,1,0:T(8,128)(2,1)}) custom-call(bf16[272,128]{1,0:T(8,128)(2,1)} %maximum_maximum_fusion.kv_ref, bf16[80,640]{1,0:T(8,128)(2,1)} %bitcast.36), custom_call_target="tpu_custom_call" | custom-call | tf_op jit(solution)/shard_map/gather_blocks/pallas_call | solution.py:155
  52.4 1.2 select_bitcast_fusion
  53.6 8.0 %all-to-all-start = ((bf16[2,2,64,16,128]{4,3,1,0,2:T(8,128)(2,1)}), bf16[2,2,64,16,128]{4,3,1,0,2:T(8,128)(2,1)S(1)}, u32[]{:S(2)}, u32[]{:S(2)}) async-start(bf16[2,2,64,16,128]{4,3,1,0,2:T(8,128)(2,1)} %select_bitcast_fusion), calls=%async_computation | async-start | bytes 2097152 | tf_op jit(solution)/shard_map/all_to_all | solution.py:347
  61.6 5.0 %attend.1.x_ref = bf16[128,640]{1,0:T(8,128)(2,1)} custom-call(bf16[128,640]{1,0:T(8,128)(2,1)} %q_ref.1, s32[1,128]{1,0:T(1,128)} %bitcast.37, bf16[64,272,128]{2,1,0:T(8,128)(2,1)} %get-tuple-element.9.kv_ref), custom_call_target="tpu_custom_call" | custom-call | bytes 100000000 | tf_op jit(solution)/shard_map/attend/pallas_call | solution.py:291
  66.5 47.7 %ring_gather.1 = bf16[8,128,640]{2,1,0:T(8,128)(2,1)} custom-call(bf16[128,640]{1,0:T(8,128)(2,1)} %attend.1.x_ref), custom_call_target="tpu_custom_call" | custom-call | tf_op jit(solution)/shard_map/ring_gather/pallas_call | solution.py:215
  114.3 0.0 all-to-all-done
  114.3 3.7 %convolution_convert_fusion = bf16[1024,640]{1,0:T(8,128)(2,1)} fusion(bf16[1024,640]{1,0:T(8,128)(2,1)} %bitcast.35, bf16[640,640]{1,0:T(8,128)(2,1)S(1)} %bitcast.38), kind=kOutput, calls=%fused_computation.3 | convolution fusion | flops 839516160 | bytes 3440640 | tf_op jit(solution)/shard_map/dot_general | solution.py:352
  118.0 4.8 %all-to-all-start.1 = ((bf16[8,128,640]{2,1,0:T(8,128)(2,1)}), bf16[8,128,640]{2,1,0:T(8,128)(2,1)S(1)}, u32[]{:S(2)}, u32[]{:S(2)}) async-start(bf16[8,128,640]{2,1,0:T(8,128)(2,1)} %bitcast.34), calls=%async_computation.1 | async-start | bytes 2621440 | tf_op jit(solution)/shard_map/all_to_all | solution.py:358
  122.8 0.6 dynamic_slice.10
  123.4 0.6 dynamic_slice.11
  125.3 0.7 iota_compare_fusion.3
  125.9 11.3 %all-to-all-done.1 = bf16[8,128,640]{2,1,0:T(8,128)(2,1)S(1)} async-done(((bf16[8,128,640]{2,1,0:T(8,128)(2,1)}), bf16[8,128,640]{2,1,0:T(8,128)(2,1)S(1)}, u32[]{:S(2)}, u32[]{:S(2)}) %all-to-all-start.1) | async-done | bytes 1310752 | tf_op jit(solution)/shard_map/all_to_all | solution.py:358
  137.2 0.2 reduce_sum.48
  137.4 0.0 copy-start.1
  137.4 5.6 %collective-permute-start = (bf16[128,640]{1,0:T(8,128)(2,1)S(1)}, bf16[128,640]{1,0:T(8,128)(2,1)S(1)}, u32[]{:S(2)}, u32[]{:S(2)}) collective-permute-start(bf16[128,640]{1,0:T(8,128)(2,1)S(1)} %reduce_sum.48), channel_id=1, source_target_pairs={{0,0},{1,64},{2,128},{3,192},{4,256},{5,320},{6,384},{7,448},{8,8}... | collective-permute-start | bytes 491528 | tf_op jit(solution)/shard_map/ppermute | solution.py:368
  143.0 1.5 bitcast_select_fusion
  144.5 8.0 %collective-permute-done = bf16[128,640]{1,0:T(8,128)(2,1)S(1)} collective-permute-done((bf16[128,640]{1,0:T(8,128)(2,1)S(1)}, bf16[128,640]{1,0:T(8,128)(2,1)S(1)}, u32[]{:S(2)}, u32[]{:S(2)}) %collective-permute-start) | collective-permute-done | bytes 163872 | tf_op jit(solution)/shard_map/ppermute | solution.py:368
  152.5 0.7 add_convert_fusion
  (11 shorter events, 0.1 us)
Async XLA Ops:
  0.6 1.7 %copy-start = (bf16[2,2,32,16,128]{4,3,2,1,0:T(8,128)(2,1)S(1)}, bf16[2,2,32,16,128]{4,3,2,1,0:T(8,128)(2,1)}, u32[]{:S(2)}) copy-start(bf16[2,2,32,16,128]{4,3,2,1,0:T(8,128)(2,1)} %param.15) | copy-start | bytes 1572868
  0.6 2.5 %copy-start.2 = (bf16[128,128]{1,0:T(8,128)(2,1)S(1)}, bf16[128,128]{1,0:T(8,128)(2,1)}, u32[]{:S(2)}) copy-start(bf16[128,128]{1,0:T(8,128)(2,1)} %param.11) | copy-start | bytes 98308
  0.7 2.5 %copy-start.3 = (bf16[128,128]{1,0:T(8,128)(2,1)S(1)}, bf16[128,128]{1,0:T(8,128)(2,1)}, u32[]{:S(2)}) copy-start(bf16[128,128]{1,0:T(8,128)(2,1)} %param.10) | copy-start | bytes 98308
  53.6 60.6 %all-to-all-start = ((bf16[2,2,64,16,128]{4,3,1,0,2:T(8,128)(2,1)}), bf16[2,2,64,16,128]{4,3,1,0,2:T(8,128)(2,1)S(1)}, u32[]{:S(2)}, u32[]{:S(2)}) async-start(bf16[2,2,64,16,128]{4,3,1,0,2:T(8,128)(2,1)} %select_bitcast_fusion), calls=%async_computation | async-start | bytes 2097152 | tf_op jit(solution)/shard_map/all_to_all | solution.py:347
  66.5 47.7 %copy-start.4 = (bf16[8,80,640]{2,1,0:T(8,128)(2,1)S(1)}, bf16[8,80,640]{2,1,0:T(8,128)(2,1)}, u32[]{:S(2)}) copy-start(bf16[8,80,640]{2,1,0:T(8,128)(2,1)} %get-tuple-element.12) | copy-start | bytes 2457604
  118.0 19.2 %all-to-all-start.1 = ((bf16[8,128,640]{2,1,0:T(8,128)(2,1)}), bf16[8,128,640]{2,1,0:T(8,128)(2,1)S(1)}, u32[]{:S(2)}, u32[]{:S(2)}) async-start(bf16[8,128,640]{2,1,0:T(8,128)(2,1)} %bitcast.34), calls=%async_computation.1 | async-start | bytes 2621440 | tf_op jit(solution)/shard_map/all_to_all | solution.py:358
  137.4 15.1 %copy-start.1 = (bf16[128,640]{1,0:T(8,128)(2,1)S(1)}, bf16[128,640]{1,0:T(8,128)(2,1)}, u32[]{:S(2)}) copy-start(bf16[128,640]{1,0:T(8,128)(2,1)} %param.13) | copy-start | bytes 491524
  137.4 15.1 %collective-permute-start = (bf16[128,640]{1,0:T(8,128)(2,1)S(1)}, bf16[128,640]{1,0:T(8,128)(2,1)S(1)}, u32[]{:S(2)}, u32[]{:S(2)}) collective-permute-start(bf16[128,640]{1,0:T(8,128)(2,1)S(1)} %reduce_sum.48), channel_id=1, source_target_pairs={{0,0},{1,64},{2,128},{3,192},{4,256},{5,320},{6,384},{7,448},{8,8}... | collective-permute-start | bytes 491528 | tf_op jit(solution)/shard_map/ppermute | solution.py:368

commit v4 on v3

--- a/solution.py
+++ b/solution.py
@@ -225,6 +225,53 @@
         ],
         compiler_params=pltpu.CompilerParams(collective_id=1, has_side_effects=True),
     )(x)
+
+
+def head_sum_kernel(part_ref, out_ref, held, send_sem, recv_sem):
+    place = lax.axis_index("head")
+    count = part_ref.shape[0]
+    barrier = pltpu.get_barrier_semaphore()
+    for d in range(1, count):
+        pl.semaphore_signal(
+            barrier, inc=1, device_id={"head": (place + d) % count}, device_id_type=MESH
+        )
+    pl.semaphore_wait(barrier, count - 1)
+    copies = {}
+    for d in (4, 3, 5, 2, 6, 1, 7):
+        to = (place + d) % count
+        copies[d] = pltpu.make_async_remote_copy(
+            src_ref=part_ref.at[to],
+            dst_ref=held.at[place],
+            send_sem=send_sem.at[d - 1],
+            recv_sem=recv_sem.at[d - 1],
+            device_id={"head": to},
+            device_id_type=MESH,
+        )
+        copies[d].start()
+    total = part_ref[place].astype(jnp.float32)
+    for d in (1, 7, 2, 6, 3, 5, 4):
+        copies[d].wait_recv()
+        total = total + held[(place + count - d) % count].astype(jnp.float32)
+    out_ref[...] = total.astype(out_ref.dtype)
+    for copy in copies.values():
+        copy.wait_send()
+
+
+def head_sum(parts):
+    return pl.pallas_call(
+        head_sum_kernel,
+        name="head_sum",
+        out_shape=jax.ShapeDtypeStruct(parts.shape[1:], parts.dtype),
+        in_specs=[pl.BlockSpec(memory_space=pltpu.VMEM)],
+        out_specs=pl.BlockSpec(memory_space=pltpu.VMEM),
+        scratch_shapes=[
+            pltpu.VMEM(parts.shape, parts.dtype),
+            pltpu.SemaphoreType.DMA((7,)),
+            pltpu.SemaphoreType.DMA((7,)),
+        ],
+        cost_estimate=pl.CostEstimate(flops=0, bytes_accessed=100_000_000, transcendentals=0),
+        compiler_params=pltpu.CompilerParams(collective_id=2, has_side_effects=True),
+    )(parts)
 
 
 def attention_kernel(q_ref, seg_ref, kv_ref, out_ref, qt_ref, top_ref, sum_ref, acc_ref):
@@ -343,11 +390,10 @@
     outgoing = jnp.where(
         sending.reshape(-1)[None, None, :, None, None], picked, jnp.zeros_like(picked)
     )
-    outgoing, kv_all = lax.optimization_barrier((outgoing, kv_all))
-    incoming = lax.all_to_all(outgoing, "seq", split_axis=2, concat_axis=2, tiled=True)
     attention = attend(block_query_rows, stretch_segments[None, :], kv_all)
     attention_all = ring_gather(attention)
-    attention_all, incoming = lax.optimization_barrier((attention_all, incoming))
+    outgoing, attention_all = lax.optimization_barrier((outgoing, attention_all))
+    incoming = lax.all_to_all(outgoing, "seq", split_axis=2, concat_axis=2, tiled=True)
     rows, width = attention.shape
     partial_sums = lax.dot_general(
         attention_all.reshape(Z * rows, width),
@@ -355,10 +401,7 @@
         (((1,), (1,)), ((), ())),
         preferred_element_type=jnp.float32,
     ).astype(jnp.bfloat16)
-    parts = lax.all_to_all(
-        partial_sums.reshape(Z, rows, width), "head", split_axis=0, concat_axis=0, tiled=True
-    )
-    total = jnp.sum(parts.astype(jnp.float32), axis=0).astype(jnp.bfloat16)
+    total = head_sum(partial_sums.reshape(Z, rows, width))
     pairs = [
         ((z * 8 + rest) * head_count + h, (h * 8 + rest) * head_count + z)
         for z in range(Z)

time: 153 us -> 160 us (1.046); the launches traced: 153 us -> 159 us
  Pallas kernels: 101 us -> 121 us
  waiting for transfers between devices: 19.2 us -> 9.51 us
  starting transfers between devices: 18.3 us -> 13.3 us
    pallas_call x0 -> x1, Pallas kernels: none -> 35 us  [head_sum(): pl.pallas_call(head_sum_kernel, name='head_sum', out_shape=jax.ShapeDtype...]
    pallas_call x1, Pallas kernels: 47.7 us -> 32.6 us  [ring_gather(): pl.pallas_call(ring_kernel, name='ring_gather', out_shape=jax.ShapeDtypeS...]
    all_to_all x1 -> x0, waiting for transfers between devices: 11.3 us -> none  [on_device(): lax.all_to_all(partial_sums.reshape(Z, rows, width), 'head', split_axis=0...]
    all_to_all x1 -> x0, starting transfers between devices: 4.77 us -> none  [on_device(): lax.all_to_all(partial_sums.reshape(Z, rows, width), 'head', split_axis=0...]
  transfers between devices with their start and end apart: 3 -> 2, of which waited for: 2 -> 1; matrix products, arithmetic and copies ran while one was open for 2% -> 4% of each run, Pallas kernels for 34% -> 22%
where the time goes in v4:
time: 160 us; the launch traced here: 159 us
  Pallas kernels  121 us (76%)
  starting transfers between devices  13.3 us (8%)
  waiting for transfers between devices  9.51 us (6%)
  other arithmetic  7.25 us (5%)
  matrix products  3.57 us (2%)
  local copies, waits for them, and re-layouts  1.99 us (1%)
  between operations  1.88 us (1%)
    pallas_call x1, Pallas kernels, gather_blocks(): pl.pallas_call(gather_kernel, name='gather_blocks', out_shape=(jax.ShapeD...  48.5 us
    pallas_call x1, Pallas kernels, head_sum(): pl.pallas_call(head_sum_kernel, name='head_sum', out_shape=jax.ShapeDtype...  35 us
    pallas_call x1, Pallas kernels, ring_gather(): pl.pallas_call(ring_kernel, name='ring_gather', out_shape=jax.ShapeDtypeS...  32.6 us
    ppermute x1, waiting for transfers between devices, on_device(): mine = lax.ppermute(total, ('seq', 'head'), pairs)  9.5 us
    all_to_all x1, starting transfers between devices, on_device(): lax.all_to_all(outgoing, 'seq', split_axis=2, concat_axis=2, tiled=True)  6.75 us
    ppermute x1, starting transfers between devices, on_device(): mine = lax.ppermute(total, ('seq', 'head'), pairs)  6.58 us
    pallas_call x1, Pallas kernels, attend(): pl.pallas_call(attention_kernel, name='attend', out_shape=jax.ShapeDtypeS...  4.96 us
    dot_general x1, matrix products, on_device(): lax.dot_general(attention_all.reshape(Z * rows, width), w_all.reshape(wid...  3.57 us
  transfers between devices with their start and end apart: 2, of which 1 were waited for; matrix products, arithmetic and copies ran while one was open for 4% of the time, Pallas kernels for 22%

profile of v4, /device:TPU:6, one launch (start us, length us, event | category | flops | bytes accessed | tf_op | source)
XLA Modules:
  0.0 158.5 jit_solution(7486244255186121586)
XLA Ops:
  0.6 0.0 copy-start
  0.7 0.8 select_reduce_fusion.1
  1.6 0.8 convert_reduce_fusion
  2.3 1.5 maximum_maximum_fusion.kv_ref
  3.9 48.5 %gather_blocks.1 = (bf16[64,272,128]{2,1,0:T(8,128)(2,1)}, bf16[8,80,640]{2,1,0:T(8,128)(2,1)}) custom-call(bf16[272,128]{1,0:T(8,128)(2,1)} %maximum_maximum_fusion.kv_ref, bf16[80,640]{1,0:T(8,128)(2,1)} %bitcast.36), custom_call_target="tpu_custom_call" | custom-call | tf_op jit(solution)/shard_map/gather_blocks/pallas_call | solution.py:155
  52.3 5.0 %attend.1.x_ref = bf16[128,640]{1,0:T(8,128)(2,1)} custom-call(bf16[128,640]{1,0:T(8,128)(2,1)} %q_ref.1, s32[1,128]{1,0:T(1,128)} %bitcast.37, bf16[64,272,128]{2,1,0:T(8,128)(2,1)} %get-tuple-element.6.kv_ref), custom_call_target="tpu_custom_call" | custom-call | bytes 100000000 | tf_op jit(solution)/shard_map/attend/pallas_call | solution.py:338
  57.3 32.6 %ring_gather.1 = bf16[8,128,640]{2,1,0:T(8,128)(2,1)} custom-call(bf16[128,640]{1,0:T(8,128)(2,1)} %attend.1.x_ref), custom_call_target="tpu_custom_call" | custom-call | tf_op jit(solution)/shard_map/ring_gather/pallas_call | solution.py:215
  89.9 0.0 copy-done
  89.9 0.8 gather_fusion
  90.7 1.2 select_bitcast_fusion
  91.9 0.0 copy-start.1
  91.9 6.8 %all-to-all-start = ((bf16[2,2,64,16,128]{4,3,1,0,2:T(8,128)(2,1)}), bf16[2,2,64,16,128]{4,3,1,0,2:T(8,128)(2,1)S(1)}, u32[]{:S(2)}, u32[]{:S(2)}) async-start(bf16[2,2,64,16,128]{4,3,1,0,2:T(8,128)(2,1)} %select_bitcast_fusion), calls=%async_computation | async-start | bytes 2097152 | tf_op jit(solution)/shard_map/all_to_all | solution.py:396
  98.7 0.0 copy-done.1
  98.7 3.6 %convolution_convert_fusion = bf16[1024,640]{1,0:T(8,128)(2,1)} fusion(bf16[1024,640]{1,0:T(8,128)(2,1)S(1)} %bitcast.34, bf16[640,640]{1,0:T(8,128)(2,1)} %bitcast.38), kind=kOutput, calls=%fused_computation.3 | convolution fusion | flops 839516160 | bytes 3440640 | tf_op jit(solution)/shard_map/dot_general | solution.py:398
  102.2 35.0 %head_sum.1 = bf16[128,640]{1,0:T(8,128)(2,1)} custom-call(bf16[8,128,640]{2,1,0:T(8,128)(2,1)} %bitcast.35), custom_call_target="tpu_custom_call" | custom-call | bytes 100000000 | tf_op jit(solution)/shard_map/head_sum/pallas_call | solution.py:261
  137.3 6.6 %collective-permute-start = (bf16[128,640]{1,0:T(8,128)(2,1)}, bf16[128,640]{1,0:T(8,128)(2,1)S(1)}, u32[]{:S(2)}, u32[]{:S(2)}) collective-permute-start(bf16[128,640]{1,0:T(8,128)(2,1)} %head_sum.1), channel_id=1, source_target_pairs={{0,0},{1,64},{2,128},{3,192},{4,256},{5,320},{6,384},{7,448},{8,8}... | collective-permute-start | bytes 491528 | tf_op jit(solution)/shard_map/ppermute | solution.py:411
  143.8 0.6 dynamic_slice.10
  144.4 0.6 dynamic_slice.11
  146.1 0.7 iota_compare_fusion.3
  146.8 9.5 %collective-permute-done = bf16[128,640]{1,0:T(8,128)(2,1)S(1)} collective-permute-done((bf16[128,640]{1,0:T(8,128)(2,1)}, bf16[128,640]{1,0:T(8,128)(2,1)S(1)}, u32[]{:S(2)}, u32[]{:S(2)}) %collective-permute-start) | collective-permute-done | bytes 163872 | tf_op jit(solution)/shard_map/ppermute | solution.py:411
  156.3 0.0 copy-done.2
  156.3 0.7 add_convert_fusion
  157.0 0.0 all-to-all-done
  157.0 1.5 bitcast_select_fusion
  (5 shorter events, 0.1 us)
Async XLA Ops:
  0.6 89.3 %copy-start = (bf16[2,2,32,16,128]{4,3,2,1,0:T(8,128)(2,1)S(1)}, bf16[2,2,32,16,128]{4,3,2,1,0:T(8,128)(2,1)}, u32[]{:S(2)}) copy-start(bf16[2,2,32,16,128]{4,3,2,1,0:T(8,128)(2,1)} %param.15) | copy-start | bytes 1572868
  91.9 6.8 %copy-start.1 = (bf16[8,128,640]{2,1,0:T(8,128)(2,1)S(1)}, bf16[8,128,640]{2,1,0:T(8,128)(2,1)}, u32[]{:S(2)}) copy-start(bf16[8,128,640]{2,1,0:T(8,128)(2,1)} %ring_gather.1) | copy-start | bytes 3932164
  91.9 65.1 %all-to-all-start = ((bf16[2,2,64,16,128]{4,3,1,0,2:T(8,128)(2,1)}), bf16[2,2,64,16,128]{4,3,1,0,2:T(8,128)(2,1)S(1)}, u32[]{:S(2)}, u32[]{:S(2)}) async-start(bf16[2,2,64,16,128]{4,3,1,0,2:T(8,128)(2,1)} %select_bitcast_fusion), calls=%async_computation | async-start | bytes 2097152 | tf_op jit(solution)/shard_map/all_to_all | solution.py:396
  102.2 54.1 %copy-start.2 = (bf16[128,640]{1,0:T(8,128)(2,1)S(1)}, bf16[128,640]{1,0:T(8,128)(2,1)}, u32[]{:S(2)}) copy-start(bf16[128,640]{1,0:T(8,128)(2,1)} %param.13) | copy-start | bytes 491524
  137.3 19.1 %collective-permute-start = (bf16[128,640]{1,0:T(8,128)(2,1)}, bf16[128,640]{1,0:T(8,128)(2,1)S(1)}, u32[]{:S(2)}, u32[]{:S(2)}) collective-permute-start(bf16[128,640]{1,0:T(8,128)(2,1)} %head_sum.1), channel_id=1, source_target_pairs={{0,0},{1,64},{2,128},{3,192},{4,256},{5,320},{6,384},{7,448},{8,8}... | collective-permute-start | bytes 491528 | tf_op jit(solution)/shard_map/ppermute | solution.py:411

commit v5 on v4

--- a/solution.py
+++ b/solution.py
@@ -227,15 +227,29 @@
     )(x)
 
 
-def head_sum_kernel(part_ref, out_ref, held, send_sem, recv_sem):
-    place = lax.axis_index("head")
+def head_sum_kernel(
+    part_ref, residual_ref, out_ref, held, total_ref, arrived, send_sem, recv_sem, swap_sem
+):
+    me, place = lax.axis_index("seq"), lax.axis_index("head")
+    z = me // 8
     count = part_ref.shape[0]
+    mirror = {"seq": place * 8 + me % 8, "head": z}
+    away = z != place
     barrier = pltpu.get_barrier_semaphore()
     for d in range(1, count):
         pl.semaphore_signal(
             barrier, inc=1, device_id={"head": (place + d) % count}, device_id_type=MESH
         )
-    pl.semaphore_wait(barrier, count - 1)
+
+    @pl.when(away)
+    def _():
+        pl.semaphore_signal(barrier, inc=1, device_id=mirror, device_id_type=MESH)
+        pl.semaphore_wait(barrier, count)
+
+    @pl.when(jnp.logical_not(away))
+    def _():
+        pl.semaphore_wait(barrier, count - 1)
+
     copies = {}
     for d in (4, 3, 5, 2, 6, 1, 7):
         to = (place + d) % count
@@ -252,26 +266,50 @@
     for d in (1, 7, 2, 6, 3, 5, 4):
         copies[d].wait_recv()
         total = total + held[(place + count - d) % count].astype(jnp.float32)
-    out_ref[...] = total.astype(out_ref.dtype)
+    total_ref[...] = total.astype(total_ref.dtype)
     for copy in copies.values():
         copy.wait_send()
 
-
-def head_sum(parts):
+    @pl.when(away)
+    def _():
+        swap = pltpu.make_async_remote_copy(
+            src_ref=total_ref,
+            dst_ref=arrived,
+            send_sem=swap_sem.at[0],
+            recv_sem=swap_sem.at[1],
+            device_id=mirror,
+            device_id_type=MESH,
+        )
+        swap.start()
+        swap.wait()
+        mine = residual_ref[...].astype(jnp.float32) + arrived[...].astype(jnp.float32)
+        out_ref[...] = mine.astype(out_ref.dtype)
+
+    @pl.when(jnp.logical_not(away))
+    def _():
+        mine = residual_ref[...].astype(jnp.float32) + total_ref[...].astype(jnp.float32)
+        out_ref[...] = mine.astype(out_ref.dtype)
+
+
+def head_sum(parts, residual):
+    block = pltpu.VMEM(residual.shape, residual.dtype)
     return pl.pallas_call(
         head_sum_kernel,
         name="head_sum",
-        out_shape=jax.ShapeDtypeStruct(parts.shape[1:], parts.dtype),
-        in_specs=[pl.BlockSpec(memory_space=pltpu.VMEM)],
+        out_shape=jax.ShapeDtypeStruct(residual.shape, residual.dtype),
+        in_specs=[pl.BlockSpec(memory_space=pltpu.VMEM)] * 2,
         out_specs=pl.BlockSpec(memory_space=pltpu.VMEM),
         scratch_shapes=[
             pltpu.VMEM(parts.shape, parts.dtype),
+            block,
+            block,
             pltpu.SemaphoreType.DMA((7,)),
             pltpu.SemaphoreType.DMA((7,)),
+            pltpu.SemaphoreType.DMA((2,)),
         ],
         cost_estimate=pl.CostEstimate(flops=0, bytes_accessed=100_000_000, transcendentals=0),
         compiler_params=pltpu.CompilerParams(collective_id=2, has_side_effects=True),
-    )(parts)
+    )(parts, residual)
 
 
 def attention_kernel(q_ref, seg_ref, kv_ref, out_ref, qt_ref, top_ref, sum_ref, acc_ref):
@@ -363,7 +401,6 @@
     request_owner,
 ):
     seq_count = lax.axis_size("seq")
-    head_count = lax.axis_size("head")
     seq_place = lax.axis_index("seq")
     ids = jnp.arange(REQUESTS, dtype=jnp.int32)
     before = jnp.sum((stretch_segments[None, :] < ids[:, None]).astype(jnp.float32), axis=1)
@@ -390,10 +427,11 @@
     outgoing = jnp.where(
         sending.reshape(-1)[None, None, :, None, None], picked, jnp.zeros_like(picked)
     )
+    outgoing, kv_all = lax.optimization_barrier((outgoing, kv_all))
+    incoming = lax.all_to_all(outgoing, "seq", split_axis=2, concat_axis=2, tiled=True)
     attention = attend(block_query_rows, stretch_segments[None, :], kv_all)
     attention_all = ring_gather(attention)
-    outgoing, attention_all = lax.optimization_barrier((outgoing, attention_all))
-    incoming = lax.all_to_all(outgoing, "seq", split_axis=2, concat_axis=2, tiled=True)
+    attention_all, incoming = lax.optimization_barrier((attention_all, incoming))
     rows, width = attention.shape
     partial_sums = lax.dot_general(
         attention_all.reshape(Z * rows, width),
@@ -401,15 +439,7 @@
         (((1,), (1,)), ((), ())),
         preferred_element_type=jnp.float32,
     ).astype(jnp.bfloat16)
-    total = head_sum(partial_sums.reshape(Z, rows, width))
-    pairs = [
-        ((z * 8 + rest) * head_count + h, (h * 8 + rest) * head_count + z)
-        for z in range(Z)
-        for rest in range(8)
-        for h in range(head_count)
-    ]
-    mine = lax.ppermute(total, ("seq", "head"), pairs)
-    layer_out = (residual.astype(jnp.float32) + mine.astype(jnp.float32)).astype(jnp.bfloat16)
+    layer_out = head_sum(partial_sums.reshape(Z, rows, width), residual)
     layers, pair_kv, _, page_len, width = incoming.shape
     arranged = jnp.swapaxes(
         incoming.reshape(layers, pair_kv, seq_count, per_pair, page_len, width), 2, 3

time: 160 us -> 156 us (0.975)
  Pallas kernels: 121 us -> 133 us
  waiting for transfers between devices: 9.51 us -> 0.01 us
  starting transfers between devices: 13.3 us -> 7.97 us
    pallas_call x1, Pallas kernels: 32.6 us -> 45.5 us  [ring_gather(): pl.pallas_call(ring_kernel, name='ring_gather', out_shape=jax.ShapeDtypeS...]
    ppermute x1 -> x0, waiting for transfers between devices: 9.5 us -> none  [on_device(): mine = lax.ppermute(total, ('seq', 'head'), pairs)]
    ppermute x1 -> x0, starting transfers between devices: 6.58 us -> none  [on_device(): mine = lax.ppermute(total, ('seq', 'head'), pairs)]
  transfers between devices with their start and end apart: 2 -> 1, of which waited for: 1 -> 0; matrix products, arithmetic and copies ran while one was open for 4% -> 1% of each run, Pallas kernels for 22% -> 32%
where the time goes in v5:
time: 156 us; the launch traced here: 155 us
  Pallas kernels  133 us (85%)
  starting transfers between devices  7.97 us (5%)
  other arithmetic  5.72 us (4%)
  matrix products  3.75 us (2%)
  local copies, waits for them, and re-layouts  2.7 us (2%)
  between operations  2.1 us (1%)
    pallas_call x1, Pallas kernels, gather_blocks(): pl.pallas_call(gather_kernel, name='gather_blocks', out_shape=(jax.ShapeD...  48.5 us
    pallas_call x1, Pallas kernels, ring_gather(): pl.pallas_call(ring_kernel, name='ring_gather', out_shape=jax.ShapeDtypeS...  45.5 us
    pallas_call x1, Pallas kernels, head_sum(): pl.pallas_call(head_sum_kernel, name='head_sum', out_shape=jax.ShapeDtype...  34.3 us
    all_to_all x1, starting transfers between devices, on_device(): lax.all_to_all(outgoing, 'seq', split_axis=2, concat_axis=2, tiled=True)  7.97 us
    pallas_call x1, Pallas kernels, attend(): pl.pallas_call(attention_kernel, name='attend', out_shape=jax.ShapeDtypeS...  4.96 us
    dot_general x1, matrix products, on_device(): lax.dot_general(attention_all.reshape(Z * rows, width), w_all.reshape(wid...  3.75 us
  transfers between devices with their start and end apart: 1, of which 0 were waited for; matrix products, arithmetic and copies ran while one was open for 1% of the time, Pallas kernels for 32%

profile of v5, /device:TPU:6, one launch (start us, length us, event | category | flops | bytes accessed | tf_op | source)
XLA Modules:
  0.0 155.5 jit_solution(6900534673623290734)
XLA Ops:
  0.6 0.0 copy-start
  0.6 0.0 copy-start.2
  0.7 0.0 copy-start.3
  0.7 0.8 select_reduce_fusion.1
  1.6 0.8 convert_reduce_fusion
  2.4 0.0 copy-done
  2.4 0.8 gather_fusion
  3.2 0.0 copy-done.2
  3.2 0.0 copy-done.3
  3.2 0.7 maximum_maximum_fusion.kv_ref
  3.9 48.5 %gather_blocks.1 = (bf16[64,272,128]{2,1,0:T(8,128)(2,1)}, bf16[8,80,640]{2,1,0:T(8,128)(2,1)}) custom-call(bf16[272,128]{1,0:T(8,128)(2,1)} %maximum_maximum_fusion.kv_ref, bf16[80,640]{1,0:T(8,128)(2,1)} %bitcast.36), custom_call_target="tpu_custom_call" | custom-call | tf_op jit(solution)/shard_map/gather_blocks/pallas_call | solution.py:155
  52.4 1.2 select_bitcast_fusion
  53.6 8.0 %all-to-all-start = ((bf16[2,2,64,16,128]{4,3,1,0,2:T(8,128)(2,1)}), bf16[2,2,64,16,128]{4,3,1,0,2:T(8,128)(2,1)S(1)}, u32[]{:S(2)}, u32[]{:S(2)}) async-start(bf16[2,2,64,16,128]{4,3,1,0,2:T(8,128)(2,1)} %select_bitcast_fusion), calls=%async_computation | async-start | bytes 2097152 | tf_op jit(solution)/shard_map/all_to_all | solution.py:431
  61.6 0.6 dynamic_slice.10
  62.2 0.6 dynamic_slice.11
  64.1 5.0 %attend.1.x_ref = bf16[128,640]{1,0:T(8,128)(2,1)} custom-call(bf16[128,640]{1,0:T(8,128)(2,1)} %q_ref.1, s32[1,128]{1,0:T(1,128)} %bitcast.37, bf16[64,272,128]{2,1,0:T(8,128)(2,1)} %get-tuple-element.9.kv_ref), custom_call_target="tpu_custom_call" | custom-call | bytes 100000000 | tf_op jit(solution)/shard_map/attend/pallas_call | solution.py:376
  69.1 45.5 %ring_gather.1 = bf16[8,128,640]{2,1,0:T(8,128)(2,1)} custom-call(bf16[128,640]{1,0:T(8,128)(2,1)} %attend.1.x_ref), custom_call_target="tpu_custom_call" | custom-call | tf_op jit(solution)/shard_map/ring_gather/pallas_call | solution.py:215
  114.6 0.6 iota_compare_fusion.3
  115.2 0.0 all-to-all-done
  115.2 3.7 %convolution_convert_fusion = bf16[1024,640]{1,0:T(8,128)(2,1)} fusion(bf16[1024,640]{1,0:T(8,128)(2,1)} %bitcast.34, bf16[640,640]{1,0:T(8,128)(2,1)S(1)} %bitcast.38), kind=kOutput, calls=%fused_computation.3 | convolution fusion | flops 839516160 | bytes 3440640 | tf_op jit(solution)/shard_map/dot_general | solution.py:436
  119.0 34.3 %head_sum.1 = bf16[128,640]{1,0:T(8,128)(2,1)} custom-call(bf16[8,128,640]{2,1,0:T(8,128)(2,1)} %bitcast.35, bf16[128,640]{1,0:T(8,128)(2,1)} %residual_ref.1), custom_call_target="tpu_custom_call" | custom-call | bytes 100000000 | tf_op jit(solution)/shard_map/head_sum/pallas_call | solution.py:296
  153.3 1.5 bitcast_select_fusion
  154.8 0.0 copy-done.1
  154.8 0.7 copy.15
  (7 shorter events, 0.1 us)
Async XLA Ops:
  0.6 1.7 %copy-start = (bf16[2,2,32,16,128]{4,3,2,1,0:T(8,128)(2,1)S(1)}, bf16[2,2,32,16,128]{4,3,2,1,0:T(8,128)(2,1)}, u32[]{:S(2)}) copy-start(bf16[2,2,32,16,128]{4,3,2,1,0:T(8,128)(2,1)} %param.15) | copy-start | bytes 1572868
  0.6 2.5 %copy-start.2 = (bf16[128,128]{1,0:T(8,128)(2,1)S(1)}, bf16[128,128]{1,0:T(8,128)(2,1)}, u32[]{:S(2)}) copy-start(bf16[128,128]{1,0:T(8,128)(2,1)} %param.11) | copy-start | bytes 98308
  0.7 2.5 %copy-start.3 = (bf16[128,128]{1,0:T(8,128)(2,1)S(1)}, bf16[128,128]{1,0:T(8,128)(2,1)}, u32[]{:S(2)}) copy-start(bf16[128,128]{1,0:T(8,128)(2,1)} %param.10) | copy-start | bytes 98308
  53.6 61.6 %all-to-all-start = ((bf16[2,2,64,16,128]{4,3,1,0,2:T(8,128)(2,1)}), bf16[2,2,64,16,128]{4,3,1,0,2:T(8,128)(2,1)S(1)}, u32[]{:S(2)}, u32[]{:S(2)}) async-start(bf16[2,2,64,16,128]{4,3,1,0,2:T(8,128)(2,1)} %select_bitcast_fusion), calls=%async_computation | async-start | bytes 2097152 | tf_op jit(solution)/shard_map/all_to_all | solution.py:431
  69.1 46.1 %copy-start.4 = (bf16[8,80,640]{2,1,0:T(8,128)(2,1)S(1)}, bf16[8,80,640]{2,1,0:T(8,128)(2,1)}, u32[]{:S(2)}) copy-start(bf16[8,80,640]{2,1,0:T(8,128)(2,1)} %get-tuple-element.12) | copy-start | bytes 2457604
  153.3 1.5 copy-start.1

commit v6 on v3

--- a/solution.py
+++ b/solution.py
@@ -344,10 +344,10 @@
         sending.reshape(-1)[None, None, :, None, None], picked, jnp.zeros_like(picked)
     )
     outgoing, kv_all = lax.optimization_barrier((outgoing, kv_all))
-    incoming = lax.all_to_all(outgoing, "seq", split_axis=2, concat_axis=2, tiled=True)
+    early = lax.all_to_all(outgoing[:1], "seq", split_axis=2, concat_axis=2, tiled=True)
     attention = attend(block_query_rows, stretch_segments[None, :], kv_all)
     attention_all = ring_gather(attention)
-    attention_all, incoming = lax.optimization_barrier((attention_all, incoming))
+    attention_all, early = lax.optimization_barrier((attention_all, early))
     rows, width = attention.shape
     partial_sums = lax.dot_general(
         attention_all.reshape(Z * rows, width),
@@ -358,6 +358,9 @@
     parts = lax.all_to_all(
         partial_sums.reshape(Z, rows, width), "head", split_axis=0, concat_axis=0, tiled=True
     )
+    parts, outgoing = lax.optimization_barrier((parts, outgoing))
+    late = lax.all_to_all(outgoing[1:], "seq", split_axis=2, concat_axis=2, tiled=True)
+    incoming = jnp.concatenate([early, late], axis=0)
     total = jnp.sum(parts.astype(jnp.float32), axis=0).astype(jnp.bfloat16)
     pairs = [
         ((z * 8 + rest) * head_count + h, (h * 8 + rest) * head_count + z)

time: 153 us -> 163 us (1.065)
  blocking collectives: 0 us -> 18.9 us
  Pallas kernels: 101 us -> 87.3 us
  starting transfers between devices: 18.3 us -> 24.2 us
  local copies, waits for them, and re-layouts: 2 us -> 3.69 us
    all_to_all x0 -> x1, blocking collectives: none -> 18.9 us  [on_device(): lax.all_to_all(partial_sums.reshape(Z, rows, width), 'head', split_axis=0...]
    pallas_call x1, Pallas kernels: 47.7 us -> 33.9 us  [ring_gather(): pl.pallas_call(ring_kernel, name='ring_gather', out_shape=jax.ShapeDtypeS...]
    all_to_all x2, waiting for transfers between devices: 11.3 us -> 0.01 us  [the longest x1 0.01 us: on_device(): lax.all_to_all(outgoing[:1], 'seq', split_axis=2, concat_axis=2, tiled=True)]
    ppermute x1, waiting for transfers between devices: 7.98 us -> 18.3 us  [on_device(): mine = lax.ppermute(total, ('seq', 'head'), pairs)]
    all_to_all x2, starting transfers between devices: 12.7 us -> 16.5 us  [the longest x1 8.57 us: on_device(): lax.all_to_all(outgoing[1:], 'seq', split_axis=2, concat_axis=2, tiled=True)]
    ppermute x1, starting transfers between devices: 5.58 us -> 7.61 us  [on_device(): mine = lax.ppermute(total, ('seq', 'head'), pairs)]
    slice x0 -> x2, local copies, waits for them, and re-layouts: none -> 1.66 us  [the longest x1 0.83 us: on_device(): outgoing[:1]]
  transfers between devices with their start and end apart: 3 -> 3, of which waited for: 2 -> 1; matrix products, arithmetic and copies ran while one was open for 2% -> 2% of each run, Pallas kernels for 34% -> 24%
where the time goes in v6:
time: 163 us
  Pallas kernels  87.3 us (54%)
  starting transfers between devices  24.2 us (15%)
  blocking collectives  18.9 us (12%)
  waiting for transfers between devices  18.3 us (11%)
  other arithmetic  5.78 us (4%)
  local copies, waits for them, and re-layouts  3.69 us (2%)
  matrix products  2.64 us (2%)
  between operations  2.09 us (1%)
    pallas_call x1, Pallas kernels, gather_blocks(): pl.pallas_call(gather_kernel, name='gather_blocks', out_shape=(jax.ShapeD...  48.5 us
    pallas_call x1, Pallas kernels, ring_gather(): pl.pallas_call(ring_kernel, name='ring_gather', out_shape=jax.ShapeDtypeS...  33.9 us
    all_to_all x1, blocking collectives, on_device(): lax.all_to_all(partial_sums.reshape(Z, rows, width), 'head', split_axis=0...  18.9 us
    ppermute x1, waiting for transfers between devices, on_device(): mine = lax.ppermute(total, ('seq', 'head'), pairs)  18.3 us
    all_to_all x1, starting transfers between devices, on_device(): lax.all_to_all(outgoing[1:], 'seq', split_axis=2, concat_axis=2, tiled=True)  8.57 us
    all_to_all x1, starting transfers between devices, on_device(): lax.all_to_all(outgoing[:1], 'seq', split_axis=2, concat_axis=2, tiled=True)  7.97 us
    ppermute x1, starting transfers between devices, on_device(): mine = lax.ppermute(total, ('seq', 'head'), pairs)  7.61 us
    pallas_call x1, Pallas kernels, attend(): pl.pallas_call(attention_kernel, name='attend', out_shape=jax.ShapeDtypeS...  4.95 us
  transfers between devices with their start and end apart: 3, of which 1 were waited for; matrix products, arithmetic and copies ran while one was open for 2% of the time, Pallas kernels for 24%

profile of v6, /device:TPU:6, one launch (start us, length us, event | category | flops | bytes accessed | tf_op | source)
XLA Modules:
  0.0 162.8 jit_solution(9679355836043329012)
XLA Ops:
  0.6 0.0 copy-start
  0.7 0.8 select_reduce_fusion.1
  1.6 0.8 convert_reduce_fusion
  2.4 0.8 gather_fusion
  3.2 0.7 maximum_maximum_fusion.kv_ref
  3.9 48.5 %gather_blocks.1 = (bf16[64,272,128]{2,1,0:T(8,128)(2,1)}, bf16[8,80,640]{2,1,0:T(8,128)(2,1)}) custom-call(bf16[272,128]{1,0:T(8,128)(2,1)} %maximum_maximum_fusion.kv_ref, bf16[80,640]{1,0:T(8,128)(2,1)} %bitcast.36), custom_call_target="tpu_custom_call" | custom-call | tf_op jit(solution)/shard_map/gather_blocks/pallas_call | solution.py:155
  52.4 0.2 select_bitcast_fusion
  52.6 0.8 slice.6
  53.5 8.0 %all-to-all-start = ((bf16[1,2,64,16,128]{4,3,1,0,2:T(8,128)(2,1)}), bf16[1,2,64,16,128]{4,3,1,0,2:T(8,128)(2,1)S(1)}, u32[]{:S(2)}, u32[]{:S(2)}) async-start(bf16[1,2,64,16,128]{4,3,1,0,2:T(8,128)(2,1)} %slice.6), calls=%async_computation | async-start | bytes 1048576 | tf_op jit(solution)/shard_map/all_to_all | solution.py:347
  61.4 4.9 %attend.1.x_ref = bf16[128,640]{1,0:T(8,128)(2,1)} custom-call(bf16[128,640]{1,0:T(8,128)(2,1)} %q_ref.1, s32[1,128]{1,0:T(1,128)} %bitcast.37, bf16[64,272,128]{2,1,0:T(8,128)(2,1)} %get-tuple-element.11.kv_ref), custom_call_target="tpu_custom_call" | custom-call | bytes 100000000 | tf_op jit(solution)/shard_map/attend/pallas_call | solution.py:291
  66.4 33.9 %ring_gather.1 = bf16[8,128,640]{2,1,0:T(8,128)(2,1)} custom-call(bf16[128,640]{1,0:T(8,128)(2,1)} %attend.1.x_ref), custom_call_target="tpu_custom_call" | custom-call | tf_op jit(solution)/shard_map/ring_gather/pallas_call | solution.py:215
  100.3 2.6 %convolution_convert_fusion = bf16[1024,640]{1,0:T(8,128)(2,1)S(1)} fusion(bf16[1024,640]{1,0:T(8,128)(2,1)} %bitcast.34, bf16[640,640]{1,0:T(8,128)(2,1)S(1)} %bitcast.38), kind=kOutput, calls=%fused_computation.3 | convolution fusion | flops 839516160 | bytes 3440640 | tf_op jit(solution)/shard_map/dot_general | solution.py:352
  103.0 18.9 %all_to_all.15 = bf16[8,128,640]{2,1,0:T(8,128)(2,1)S(1)} all-to-all(bf16[8,128,640]{2,1,0:T(8,128)(2,1)S(1)} %bitcast.35), channel_id=1, replica_groups=mesh['seq'=64,'head'=8] {'head'}, dimensions={0} | all-to-all | bytes 2621440 | tf_op jit(solution)/shard_map/all_to_all | solution.py:358
  121.9 0.8 slice.7
  122.7 8.6 %all-to-all-start.2 = ((bf16[1,2,64,16,128]{4,3,1,0,2:T(8,128)(2,1)}), bf16[1,2,64,16,128]{4,3,1,0,2:T(8,128)(2,1)S(1)}, u32[]{:S(2)}, u32[]{:S(2)}) async-start(bf16[1,2,64,16,128]{4,3,1,0,2:T(8,128)(2,1)} %slice.7), calls=%async_computation.2 | async-start | bytes 1048576 | tf_op jit(solution)/shard_map/all_to_all | solution.py:362
  131.3 0.2 reduce_sum.48
  131.5 7.6 %collective-permute-start = (bf16[128,640]{1,0:T(8,128)(2,1)S(1)}, bf16[128,640]{1,0:T(8,128)(2,1)S(1)}, u32[]{:S(2)}, u32[]{:S(2)}) collective-permute-start(bf16[128,640]{1,0:T(8,128)(2,1)S(1)} %reduce_sum.48), channel_id=1, source_target_pairs={{0,0},{1,64},{2,128},{3,192},{4,256},{5,320},{6,384},{7,448},{8,8}... | collective-permute-start | bytes 491528 | tf_op jit(solution)/shard_map/ppermute | solution.py:371
  139.1 0.6 dynamic_slice.10
  139.7 0.6 dynamic_slice.11
  141.6 0.7 iota_compare_fusion.3
  142.2 18.3 %collective-permute-done = bf16[128,640]{1,0:T(8,128)(2,1)S(1)} collective-permute-done((bf16[128,640]{1,0:T(8,128)(2,1)S(1)}, bf16[128,640]{1,0:T(8,128)(2,1)S(1)}, u32[]{:S(2)}, u32[]{:S(2)}) %collective-permute-start) | collective-permute-done | bytes 163872 | tf_op jit(solution)/shard_map/ppermute | solution.py:371
  160.5 0.7 add_convert_fusion
  161.2 0.1 maximum_bitcast_fusion
  161.3 1.5 bitcast_select_fusion
  (15 shorter events, 0.1 us)
Async XLA Ops:
  0.6 1.7 %copy-start = (bf16[2,2,32,16,128]{4,3,2,1,0:T(8,128)(2,1)S(1)}, bf16[2,2,32,16,128]{4,3,2,1,0:T(8,128)(2,1)}, u32[]{:S(2)}) copy-start(bf16[2,2,32,16,128]{4,3,2,1,0:T(8,128)(2,1)} %param.15) | copy-start | bytes 1572868
  0.6 2.5 %copy-start.2 = (bf16[128,128]{1,0:T(8,128)(2,1)S(1)}, bf16[128,128]{1,0:T(8,128)(2,1)}, u32[]{:S(2)}) copy-start(bf16[128,128]{1,0:T(8,128)(2,1)} %param.11) | copy-start | bytes 98308
  0.7 2.5 %copy-start.3 = (bf16[128,128]{1,0:T(8,128)(2,1)S(1)}, bf16[128,128]{1,0:T(8,128)(2,1)}, u32[]{:S(2)}) copy-start(bf16[128,128]{1,0:T(8,128)(2,1)} %param.10) | copy-start | bytes 98308
  53.5 46.8 %all-to-all-start = ((bf16[1,2,64,16,128]{4,3,1,0,2:T(8,128)(2,1)}), bf16[1,2,64,16,128]{4,3,1,0,2:T(8,128)(2,1)S(1)}, u32[]{:S(2)}, u32[]{:S(2)}) async-start(bf16[1,2,64,16,128]{4,3,1,0,2:T(8,128)(2,1)} %slice.6), calls=%async_computation | async-start | bytes 1048576 | tf_op jit(solution)/shard_map/all_to_all | solution.py:347
  66.4 33.9 %copy-start.4 = (bf16[8,80,640]{2,1,0:T(8,128)(2,1)S(1)}, bf16[8,80,640]{2,1,0:T(8,128)(2,1)}, u32[]{:S(2)}) copy-start(bf16[8,80,640]{2,1,0:T(8,128)(2,1)} %get-tuple-element.14) | copy-start | bytes 2457604
  122.7 37.8 %copy-start.1 = (bf16[128,640]{1,0:T(8,128)(2,1)S(1)}, bf16[128,640]{1,0:T(8,128)(2,1)}, u32[]{:S(2)}) copy-start(bf16[128,640]{1,0:T(8,128)(2,1)} %param.13) | copy-start | bytes 491524
  122.7 38.5 %all-to-all-start.2 = ((bf16[1,2,64,16,128]{4,3,1,0,2:T(8,128)(2,1)}), bf16[1,2,64,16,128]{4,3,1,0,2:T(8,128)(2,1)S(1)}, u32[]{:S(2)}, u32[]{:S(2)}) async-start(bf16[1,2,64,16,128]{4,3,1,0,2:T(8,128)(2,1)} %slice.7), calls=%async_computation.2 | async-start | bytes 1048576 | tf_op jit(solution)/shard_map/all_to_all | solution.py:362
  131.5 29.0 %collective-permute-start = (bf16[128,640]{1,0:T(8,128)(2,1)S(1)}, bf16[128,640]{1,0:T(8,128)(2,1)S(1)}, u32[]{:S(2)}, u32[]{:S(2)}) collective-permute-start(bf16[128,640]{1,0:T(8,128)(2,1)S(1)} %reduce_sum.48), channel_id=1, source_target_pairs={{0,0},{1,64},{2,128},{3,192},{4,256},{5,320},{6,384},{7,448},{8,8}... | collective-permute-start | bytes 491528 | tf_op jit(solution)/shard_map/ppermute | solution.py:371
